TPU v7x, 32 devices: a whole 2x2x4 slice. The times are simulated.
32 devices in a mesh: seq: 8 (over z, y), head: 4 (over x, core).
Axes of the slice: x: 2, y: 2, z: 4, core: 2. Of those that a mesh axis runs over, the one named last changes fastest.
Arguments:
- queries: bfloat16 [4096, 2048], P('seq', 'head'), may hold values from -6 to 6
- key_vectors: bfloat16 [4096, 2048], P('seq', 'head'), may hold values from -8 to 8
- value_vectors: bfloat16 [4096, 2048], P('seq', 'head'), may hold values from -40 to 40
- norm_gain: float32 [2048], P('head'), may hold values from 0.25 to 1.75
- out_weight: bfloat16 [2048, 2048], P('head'), may hold values from -0.125 to 0.125
Outputs:
- projected: bfloat16 [4096, 2048], P(('seq', 'head'))
All inputs are finite; a program needn't handle non-finite values.
Results may differ from a plain program's by a relative error of at most 0.013.
Values may be sent and summed in bfloat16 or wider, within the bound.
No kernel may reach another device: no remote copies, remote signals or barrier semaphores. Data moves between devices by JAX's collectives and lax.ppermute only.
A program may use at most 128 MiB of HBM per device.

v0:
```python
import functools

import jax
import jax.numpy as jnp
from jax import lax
from jax.experimental import pallas as pl
from jax.experimental.pallas import tpu as pltpu
from jax.sharding import PartitionSpec as P


DH = 128
DIAG = 16
F32 = jnp.float32
BF16 = jnp.bfloat16


def mm(a, b):
    return lax.dot_general(a, b, (((1,), (0,)), ((), ())), preferred_element_type=F32)


def mm_nt(a, b):
    return lax.dot_general(a, b, (((1,), (1,)), ((), ())), preferred_element_type=F32)


def mm_tn(a, b):
    return lax.dot_general(a, b, (((0,), (0,)), ((), ())), preferred_element_type=F32)


def row_col(n):
    return lax.broadcasted_iota(jnp.int32, (n, n), 0), lax.broadcasted_iota(jnp.int32, (n, n), 1)


def is_upper(bit):
    return lax.bitwise_and(lax.axis_index("seq"), bit) != 0


def columns(h):
    return slice(h * DH, (h + 1) * DH)


def call(kernel, ins, outs, flops=0, scratch=(), mib=4):
    arrays = [pltpu.with_memory_space_constraint(a, space) if space is pltpu.HBM else a for a, space in ins]
    data = sum(a.size * a.dtype.itemsize for a in arrays)
    return pl.pallas_call(
        kernel,
        in_specs=[pl.BlockSpec(memory_space=space) for a, space in ins],
        out_specs=[pl.BlockSpec(memory_space=pltpu.VMEM) for o in outs],
        out_shape=[pltpu.VMEM(shape, dtype) for shape, dtype in outs],
        scratch_shapes=list(scratch),
        compiler_params=pltpu.CompilerParams(vmem_limit_bytes=mib << 20),
        cost_estimate=pl.CostEstimate(flops=int(flops), bytes_accessed=int(data), transcendentals=0),
    )(*arrays)


def vm(*arrays):
    return [(a, pltpu.VMEM) for a in arrays]


def pack(send_ref, grams):
    heads = len(grams)
    pairs = (heads + 1) // 2
    row, col = row_col(DH)
    diagonals = []
    for p in range(pairs):
        a, b = grams[2 * p], grams[min(2 * p + 1, heads - 1)]
        send_ref[pl.ds(p * DH, DH), :] = jnp.where(row <= col, a, b).astype(BF16)
        diagonals.append(jnp.sum(jnp.where(row == col, b, 0.0), axis=0, keepdims=True))
    diagonals += [jnp.zeros((1, DH), F32)] * (DIAG - pairs)
    send_ref[pl.ds(pairs * DH, DIAG), :] = jnp.concatenate(diagonals, axis=0).astype(BF16)


def unpack(got_ref, heads):
    pairs = (heads + 1) // 2
    row, col = row_col(DH)
    diagonals = got_ref[pl.ds(pairs * DH, DIAG), :].astype(F32)
    grams = []
    for p in range(pairs):
        m = got_ref[pl.ds(p * DH, DH), :].astype(F32)
        t = m.T
        d = jnp.broadcast_to(diagonals[p : p + 1, :], (DH, DH))
        grams.append(jnp.where(row <= col, m, t))
        grams.append(jnp.where(row > col, m, jnp.where(row < col, t, d)))
    return grams[:heads]


def packed_rows(heads):
    return (heads + 1) // 2 * DH + DIAG


def sums_kernel(chunks, q_hbm, k_hbm, v_hbm, w_hbm, q_ref, k_ref, v_ref, own_ref, send_ref, *refs):
    *w_refs, sem, w_sem = refs
    rows, width = q_ref.shape
    heads = width // DH
    size = rows // chunks
    copies = []
    for c in range(chunks):
        at = pl.ds(c * size, size)
        for n, (src, dst) in enumerate(((k_hbm, k_ref), (q_hbm, q_ref), (v_hbm, v_ref))):
            copies.append(pltpu.make_async_copy(src.at[at], dst.at[at], sem.at[c, n]))
    share = w_refs[0].shape[0]
    first = lax.bitwise_and(lax.axis_index("seq"), 1) * len(w_refs)
    for n, w_ref in enumerate(w_refs):
        at = pl.multiple_of((first + n) * share, share)
        copies.append(pltpu.make_async_copy(w_hbm.at[pl.ds(at, share)], w_ref, w_sem.at[n]))
    for copy in copies:
        copy.start()
    grams = [None] * heads
    crosses = [None] * heads
    for c in range(chunks):
        at = pl.ds(c * size, size)
        copies[3 * c].wait()
        for h in range(heads):
            k = k_ref[at, columns(h)]
            gram = mm_tn(k, k)
            grams[h] = gram if c == 0 else grams[h] + gram
        copies[3 * c + 1].wait()
        copies[3 * c + 2].wait()
        for h in range(heads):
            cross = mm_tn(q_ref[at, columns(h)], v_ref[at, columns(h)])
            crosses[h] = cross if c == 0 else crosses[h] + cross
    base = packed_rows(heads)
    pack(send_ref, grams)
    for h in range(heads):
        own_ref[0, h] = grams[h]
        own_ref[1, h] = crosses[h]
        send_ref[pl.ds(base + h * DH, DH), :] = crosses[h].astype(BF16)
    for copy in copies[3 * chunks :]:
        copy.wait()


def local_sums(q, k, v, weight, share, shares):
    rows, width = q.shape
    heads = width // DH
    chunks = 2 if rows % 32 == 0 else 1
    return call(
        functools.partial(sums_kernel, chunks),
        [(a, pltpu.HBM) for a in (q, k, v, weight)],
        [((rows, width), BF16)] * 3
        + [((2, heads, DH, DH), F32), ((packed_rows(heads) + heads * DH, DH), BF16)]
        + [((share, weight.shape[1]), BF16)] * shares,
        flops=4 * rows * width * DH,
        scratch=[pltpu.SemaphoreType.DMA((chunks, 3)), pltpu.SemaphoreType.DMA((shares,))],
        mib=6,
    )


def pairs_kernel(block, q_ref, k_ref, v_ref, w_hbm, own_ref, send_ref, w_ref, w_sem):
    rest = w_ref.shape[0]
    copy = pltpu.make_async_copy(w_hbm.at[pl.ds(w_hbm.shape[0] - rest, rest)], w_ref, w_sem)
    copy.start()
    rows, width = q_ref.shape
    row, col = row_col(block)
    for h in range(width // DH):
        gram = pair = None
        for start in range(0, rows, block):
            at = pl.ds(start, block)
            q, k, v = q_ref[at, columns(h)], k_ref[at, columns(h)], v_ref[at, columns(h)]
            paired = jnp.where(row < col, mm_nt(k, q), 0.0).astype(BF16)
            here = mm_tn(k, mm(paired, v).astype(BF16))
            if start:
                here = pair + here + mm(gram.astype(BF16), mm_tn(q, v).astype(BF16))
            pair = here
            if start + block < rows:
                more = mm_tn(k, k)
                gram = gram + more if start else more
        own_ref[h] = pair
        send_ref[pl.ds(h * DH, DH), :] = pair.astype(BF16)
    copy.wait()


def local_pairs(q, k, v, weight, rest, block):
    rows, width = q.shape
    heads = width // DH
    return call(
        functools.partial(pairs_kernel, block),
        vm(q, k, v) + [(weight, pltpu.HBM)],
        [((heads, DH, DH), F32), ((heads * DH, DH), BF16), ((rest, weight.shape[1]), BF16)],
        flops=4 * rows * width * block,
        scratch=[pltpu.SemaphoreType.DMA],
    )


def union_sums_kernel(bit, first, last, got_ref, own_ref, *refs):
    refs = list(refs)
    ahead_ref = None if first else refs.pop(0)
    ahead_out, send_ref, left_ref, right_ref, came_ref = refs[:5]
    own_out = None if last else refs[5]
    heads = own_ref.shape[1]
    upper = is_upper(bit)
    weight = upper.astype(F32)
    base = packed_rows(heads)
    totals = []
    for h, gram in enumerate(unpack(got_ref, heads)):
        mine = own_ref[0, h]
        total = mine + gram
        totals.append(total)
        if not last:
            own_out[0, h] = total
        ahead_out[0, h] = weight * gram if first else ahead_ref[0, h] + weight * gram
        left_ref[h] = jnp.where(upper, gram, mine).astype(BF16)
        came_ref[h] = gram.astype(BF16)
    pack(send_ref, totals)
    for h in range(heads):
        cross = got_ref[pl.ds(base + h * DH, DH), :].astype(F32)
        mine = own_ref[1, h]
        total = mine + cross
        ahead_out[1, h] = weight * cross if first else ahead_ref[1, h] + weight * cross
        right_ref[h] = jnp.where(upper, mine, cross).astype(BF16)
        if not last:
            own_out[1, h] = total
            send_ref[pl.ds(base + h * DH, DH), :] = total.astype(BF16)


def union_sums(bit, got, own, ahead, last):
    heads = own.shape[1]
    first = ahead is None
    rows = packed_rows(heads) + (0 if last else heads * DH)
    low = ((heads, DH, DH), BF16)
    return call(
        functools.partial(union_sums_kernel, bit, first, last),
        vm(got, own) + ([] if first else vm(ahead)),
        [(own.shape, F32), ((rows, DH), BF16), low, low, low] + ([] if last else [(own.shape, F32)]),
    )


def union_pairs_kernel(bit, first, last, got_ref, own_ref, left_ref, right_ref, *refs):
    refs = list(refs)
    if not first:
        before_ref, came_ref, ahead_ref = refs[:3]
        refs = refs[3:]
    before_out, send_ref = refs[:2]
    weight = is_upper(bit).astype(F32)
    for h in range(own_ref.shape[0]):
        got = got_ref[pl.ds(h * DH, DH), :].astype(F32)
        total = own_ref[h] + got + mm(left_ref[h], right_ref[h])
        if not last:
            refs[2][h] = total
        send_ref[pl.ds(h * DH, DH), :] = total.astype(BF16)
        if first:
            before_out[h] = weight * got
        else:
            before_out[h] = before_ref[h] + weight * (got + mm(came_ref[h], ahead_ref[1, h].astype(BF16)))


def union_pairs(bit, got, own, left, right, before, came, ahead, last):
    first = before is None
    return call(
        functools.partial(union_pairs_kernel, bit, first, last),
        vm(got, own, left, right) + ([] if first else vm(before, came, ahead)),
        [(own.shape, F32), (got.shape, BF16)] + ([] if last else [(own.shape, F32)]),
        flops=own.size * 4 * DH,
    )


def ahead_kernel(bit, got_ref, ahead_ref, before_ref, gram_ref, base_ref):
    weight = is_upper(bit).astype(F32)
    heads = before_ref.shape[0]
    for h, gram in enumerate(unpack(got_ref, heads)):
        gram_ref[h] = (ahead_ref[0, h] + weight * gram).astype(BF16)
        base_ref[h] = before_ref[h] + weight * mm(gram.astype(BF16), ahead_ref[1, h].astype(BF16))


def ahead_of_device(bit, got, ahead, before):
    return call(
        functools.partial(ahead_kernel, bit),
        vm(got, ahead, before),
        [(before.shape, BF16), (before.shape, F32)],
        flops=before.size * 2 * DH,
    )


def inner_kernel(block, heads, q_ref, k_ref, v_ref, out_ref):
    rows = q_ref.shape[0]
    row, col = row_col(block)
    for n, h in enumerate(heads):
        gram = pair = None
        for start in range(0, rows, block):
            at = pl.ds(start, block)
            q, k, v = q_ref[at, columns(h)], k_ref[at, columns(h)], v_ref[at, columns(h)]
            paired = jnp.where(row < col, mm_nt(k, q), 0.0).astype(BF16)
            mixing = mm(mm_nt(q, k).astype(BF16), paired)
            if start:
                mixing = mixing + mm_nt(mm(q, gram.astype(BF16)).astype(BF16), q)
            result = mm(jnp.where(row >= col, mixing, 0.0).astype(BF16), v)
            if start:
                result = result + mm(q, pair.astype(BF16))
            out_ref[at, columns(n)] = result
            if start + block < rows:
                here = mm_tn(k, mm(paired, v).astype(BF16))
                if start:
                    here = pair + here + mm(gram.astype(BF16), mm_tn(q, v).astype(BF16))
                pair = here
                more = mm_tn(k, k)
                gram = gram + more if start else more


def inner(q, k, v, block, heads):
    rows = q.shape[0]
    return call(
        functools.partial(inner_kernel, block, heads),
        vm(q, k, v),
        [((rows, len(heads) * DH), F32)],
        flops=rows * len(heads) * DH * 8 * block,
    )[0]


def outer_kernel(block, q_ref, v_ref, gram_ref, *refs):
    *part_refs, out_ref = refs
    rows = q_ref.shape[0]
    row, col = row_col(block)
    parts = [(ref, n) for ref in part_refs for n in range(ref.shape[1] // DH)]
    for h, (part_ref, n) in enumerate(parts):
        cross = None
        for start in range(0, rows, block):
            at = pl.ds(start, block)
            q, v = q_ref[at, columns(h)], v_ref[at, columns(h)]
            state = mm(q, gram_ref[h]).astype(BF16)
            mixing = jnp.where(row >= col, mm_nt(state, q), 0.0).astype(BF16)
            result = part_ref[at, columns(n)] + mm(mixing, v)
            if start:
                result = result + mm(state, cross.astype(BF16))
            out_ref[at, columns(h)] = result
            if start + block < rows:
                more = mm_tn(q, v)
                cross = cross + more if start else more


def outer(q, v, gram, parts, block):
    rows, width = q.shape
    return call(
        functools.partial(outer_kernel, block),
        vm(q, v, gram, *parts),
        [((rows, width), F32)],
        flops=rows * width * 6 * block,
    )[0]


def normed_kernel(bit, blocks, other, q_ref, part_ref, base_ref, got_ref, gain_ref, out_ref):
    weight = is_upper(bit).astype(F32)
    size = q_ref.shape[0] // blocks
    first = lax.bitwise_xor(lax.axis_index("head"), other)
    for h in range(base_ref.shape[0]):
        pair = (base_ref[h] + weight * got_ref[pl.ds(h * DH, DH), :].astype(F32)).astype(BF16)
        for j in range(blocks // 2):
            at = pl.ds(pl.multiple_of(lax.bitwise_xor(first, j) * size, size), size)
            attended = part_ref[at, columns(h)] + mm(q_ref[at, columns(h)], pair)
            mean = jnp.mean(attended * attended, axis=-1, keepdims=True)
            normed = attended * lax.rsqrt(mean + 1e-6) * gain_ref[:, columns(h)]
            out_ref[j, :, columns(h)] = normed.astype(BF16)


def normed_blocks(bit, other, q, part, base, got, gain, blocks):
    rows, width = q.shape
    return call(
        functools.partial(normed_kernel, bit, blocks, other),
        vm(q, part, base, got, gain),
        [((blocks // 2, rows // blocks, width), BF16)],
        flops=rows * width * DH,
    )[0]


def weights_kernel(shares, *refs):
    *parts, rest_ref, out_ref = refs
    share = parts[0].shape[0]
    odd = lax.bitwise_and(lax.axis_index("seq"), 1)
    for n in range(shares):
        for first, ref in ((odd, parts[n]), (1 - odd, parts[shares + n])):
            at = pl.multiple_of((first * shares + n) * share, share)
            out_ref[pl.ds(at, share), :] = ref[...]
    out_ref[pl.ds(2 * shares * share, rest_ref.shape[0]), :] = rest_ref[...]


def join_weights(direct, neighbour, rest):
    rows = (len(direct) + len(neighbour)) * direct[0].shape[0] + rest.shape[0]
    return call(
        functools.partial(weights_kernel, len(direct)),
        vm(*direct, *neighbour, rest),
        [((rows, rest.shape[1]), BF16)],
        mib=8,
    )[0]


def project_own_kernel(kept_ref, w_ref, out_ref):
    blocks, size, width = kept_ref.shape
    kept = kept_ref[...].reshape(blocks * size, width)
    span = out_ref.shape[2]
    tile = 512 if span % 512 == 0 else span
    for start in range(0, span, tile):
        at = slice(start, start + tile)
        out_ref[:, :, at] = mm(kept, w_ref[:, at]).reshape(blocks, size, tile)


def project_own(kept, weight):
    blocks, size, width = kept.shape
    span = weight.shape[1]
    return call(
        project_own_kernel,
        vm(kept, weight),
        [((blocks, size, span), F32)],
        flops=2 * blocks * size * width * span,
        mib=8,
    )[0]


def project_kernel(index, own_ref, came_ref, w_ref, out_ref):
    span = out_ref.shape[1]
    tile = 512 if span % 512 == 0 else span
    for start in range(0, span, tile):
        at = slice(start, start + tile)
        out_ref[:, at] = (own_ref[index, :, at] + mm(came_ref[index], w_ref[:, at])).astype(out_ref.dtype)


def project(index, own, came, weight, dtype):
    _, size, span = own.shape
    return call(
        functools.partial(project_kernel, index),
        vm(own, came, weight),
        [((size, span), dtype)],
        flops=2 * size * came.shape[2] * span,
        mib=8,
    )[0]


def flip(value, axis, bit):
    count = lax.axis_size(axis)
    return lax.ppermute(value, axis, [(i, i ^ bit) for i in range(count)])


def shards(queries, key_vectors, value_vectors, norm_gain, out_weight):
    rows, width = queries.shape
    seq_count, head_count = lax.axis_size("seq"), lax.axis_size("head")
    block = 256 if rows % 256 == 0 else rows

    top = head_count // 2
    features = out_weight.shape[0]
    shares = 2
    share = features * 3 // 8 // shares // 16 * 16

    q, k, v, sums, sums_send, *weight_shares = local_sums(
        queries, key_vectors, value_vectors, out_weight, share, shares
    )
    pairs, pairs_send, weight_rest = local_pairs(
        q, k, v, out_weight, features - 2 * shares * share, block
    )
    direct = [flip(w, "head", top) for w in weight_shares]
    neighbour = [flip(w, "seq", 1) for w in direct]
    rest = flip(weight_rest, "head", top)
    heads = width // DH
    parts = [
        inner(q, k, v, block, tuple(range(at, min(at + (heads + 1) // 2, heads))))
        for at in range(0, heads, (heads + 1) // 2)
    ]
    ahead = before = None
    bit = 1
    while 2 * bit < seq_count:
        sums_got = flip(sums_send, "seq", bit)
        pairs_got = flip(pairs_send, "seq", bit)
        old = ahead
        last = 4 * bit >= seq_count
        ahead, sums_send, left, right, came, *more = union_sums(bit, sums_got, sums, ahead, last)
        before, pairs_send, *more_pairs = union_pairs(
            bit, pairs_got, pairs, left, right, before, came, old, last
        )
        if not last:
            (pairs,) = more_pairs
            (sums,) = more
        bit *= 2
    gram_got = flip(sums_send, "seq", bit)
    pairs_got = flip(pairs_send, "seq", bit)
    gram, base = ahead_of_device(bit, gram_got, ahead, before)
    part = outer(q, v, gram, parts, block)

    gain = norm_gain.reshape(1, width)
    sent = normed_blocks(bit, top, q, part, base, pairs_got, gain, head_count)
    came = flip(sent, "head", top)
    kept = normed_blocks(bit, 0, q, part, base, pairs_got, gain, head_count)
    own = project_own(kept, out_weight)
    weight_came = join_weights(direct, neighbour, rest)

    count = top
    if count == 1:
        return project(0, own, came, weight_came, BF16)
    results = {
        j: project(j, own, came, weight_came, BF16 if 2 * j >= count else F32) for j in reversed(range(count))
    }
    while count > 1:
        count //= 2
        for j in range(count):
            got = flip(results[count + j].astype(BF16), "head", count)
            results[j] = results[j].astype(F32) + got.astype(F32)
    return results[0].astype(BF16)


def solution(mesh):
    in_specs = (P("seq", "head"), P("seq", "head"), P("seq", "head"), P("head"), P("head", None))
    out_specs = P(("seq", "head"), None)

    return jax.shard_map(shards, mesh=mesh, in_specs=in_specs, out_specs=out_specs, check_vma=False)
```

profile of v0, /device:TPU:0, one launch (start us, length us, event | category | flops | bytes accessed | tf_op | source)
XLA Modules:
  0.0 46.0 jit_solution(7988900476470880142)
XLA Ops:
  0.0 2.0 %shard_map.55 = (bf16[512,512]{1,0:T(8,128)(2,1)S(1)}, bf16[512,512]{1,0:T(8,128)(2,1)S(1)}, bf16[512,512]{1,0:T(8,128)(2,1)S(1)}, f32[2,4,128,128]{3,2,1,0:T(8,...) custom-call(bf16[512,512]{1,0:T(8,128)(2,1)} %q_hbm.1, ...), custom_call_target="tpu_custom_call" | custom-call | flops 134217728 | bytes 3670016 | tf_op jit(solution)/shard_map/pallas_call | solution.py:44
  2.0 3.1 %collective-permute-start = (bf16[784,128]{1,0:T(8,128)(2,1)S(1)}, bf16[784,128]{1,0:T(8,128)(2,1)S(1)}, u32[]{:S(2)}, u32[]{:S(2)}) collective-permute-start(bf16[784,128]{1,0:T(8,128)(2,1)S(1)} %get-tuple-element.34), channel_id=1, source_target_pairs={{0,4},{4,0},{8,12},{12,8},{16,20},{20,16},{24,28},{28,24},{1,5},{5... | collective-permute-start | bytes 602120 | tf_op jit(solution)/shard_map/ppermute | solution.py:426
  5.1 1.5 %collective-permute-start.8 = (bf16[96,2048]{1,0:T(8,128)(2,1)S(1)}, bf16[96,2048]{1,0:T(8,128)(2,1)S(1)}, u32[]{:S(2)}, u32[]{:S(2)}) collective-permute-start(bf16[96,2048]{1,0:T(8,128)(2,1)S(1)} %get-tuple-element.57), channel_id=1, source_target_pairs={{0,2},{1,3},{2,0},{3,1},{4,6},{5,7},{6,4},{7,5},{8,10},{9,11},{10,... | collective-permute-start | bytes 1179656 | tf_op jit(solution)/shard_map/ppermute | solution.py:426
  6.6 0.5 %collective-permute-start.7 = (bf16[96,2048]{1,0:T(8,128)(2,1)S(1)}, bf16[96,2048]{1,0:T(8,128)(2,1)S(1)}, u32[]{:S(2)}, u32[]{:S(2)}) collective-permute-start(bf16[96,2048]{1,0:T(8,128)(2,1)S(1)} %get-tuple-element.56), channel_id=1, source_target_pairs={{0,2},{1,3},{2,0},{3,1},{4,6},{5,7},{6,4},{7,5},{8,10},{9,11},{10,... | collective-permute-start | bytes 1179656 | tf_op jit(solution)/shard_map/ppermute | solution.py:426
  7.1 2.9 %shard_map.58 = (f32[4,128,128]{2,1,0:T(8,128)S(1)}, bf16[512,128]{1,0:T(8,128)(2,1)S(1)}, bf16[128,2048]{1,0:T(8,128)(2,1)S(1)}) custom-call(bf16[512,512]{1,0:T(8,128)(2,1)S(1)} %get-tuple-element.32.q_ref, bf16[512,512]{1,0:T(8,128)(2,1)S(1)} %get-tuple-element.41.k_ref, bf16[512,512]{1,0:T(8,128)(2,1)S(1)} %get-tuple-element.33.v_ref, ...), custom_call_target="tpu_custom_call" | custom-call | flops 268435456 | bytes 3670016 | tf_op jit(solution)/shard_map/pallas_call | solution.py:44
  10.1 0.8 %shard_map.56 = (f32[2,4,128,128]{3,2,1,0:T(8,128)S(1)}, bf16[784,128]{1,0:T(8,128)(2,1)S(1)}, bf16[4,128,128]{2,1,0:T(8,128)(2,1)S(1)}, bf16[4,128,128]{2,1,0:T...) custom-call(bf16[784,128]{1,0:T(8,128)(2,1)S(1)} %collective-permute-done.got_ref, ...), custom_call_target="tpu_custom_call" | custom-call | bytes 724992 | tf_op jit(solution)/shard_map/pallas_call | solution.py:44
  10.9 2.0 %collective-permute-start.1 = (bf16[784,128]{1,0:T(8,128)(2,1)S(1)}, bf16[784,128]{1,0:T(8,128)(2,1)S(1)}, u32[]{:S(2)}, u32[]{:S(2)}) collective-permute-start(bf16[784,128]{1,0:T(8,128)(2,1)S(1)} %get-tuple-element.36), channel_id=1, source_target_pairs={{0,8},{4,12},{8,0},{12,4},{16,24},{20,28},{24,16},{28,20},{1,9},{5... | collective-permute-start | bytes 602120 | tf_op jit(solution)/shard_map/ppermute | solution.py:426
  13.0 2.0 %collective-permute-done.3.got_ref = bf16[512,128]{1,0:T(8,128)(2,1)S(1)} collective-permute-done((bf16[512,128]{1,0:T(8,128)(2,1)S(1)}, bf16[512,128]{1,0:T(8,128)(2,1)S(1)}, u32[]{:S(2)}, u32[]{:S(2)}) %collective-permute-start.3) | collective-permute-done | bytes 131104 | tf_op jit(solution)/shard_map/ppermute | solution.py:426
  15.2 1.6 %collective-permute-start.4 = (bf16[512,128]{1,0:T(8,128)(2,1)S(1)}, bf16[512,128]{1,0:T(8,128)(2,1)S(1)}, u32[]{:S(2)}, u32[]{:S(2)}) collective-permute-start(bf16[512,128]{1,0:T(8,128)(2,1)S(1)} %get-tuple-element.46), channel_id=1, source_target_pairs={{0,8},{4,12},{8,0},{12,4},{16,24},{20,28},{24,16},{28,20},{1,9},{5... | collective-permute-start | bytes 393224 | tf_op jit(solution)/shard_map/ppermute | solution.py:426
  16.8 1.5 %collective-permute-start.11 = (bf16[128,2048]{1,0:T(8,128)(2,1)S(1)}, bf16[128,2048]{1,0:T(8,128)(2,1)S(1)}, u32[]{:S(2)}, u32[]{:S(2)}) collective-permute-start(bf16[128,2048]{1,0:T(8,128)(2,1)S(1)} %get-tuple-element.58), channel_id=1, source_target_pairs={{0,2},{1,3},{2,0},{3,1},{4,6},{5,7},{6,4},{7,5},{8,10},{9,11},{10,... | collective-permute-start | bytes 1572872 | tf_op jit(solution)/shard_map/ppermute | solution.py:426
  18.5 1.7 %collective-permute-done.4.got_ref = bf16[512,128]{1,0:T(8,128)(2,1)S(1)} collective-permute-done((bf16[512,128]{1,0:T(8,128)(2,1)S(1)}, bf16[512,128]{1,0:T(8,128)(2,1)S(1)}, u32[]{:S(2)}, u32[]{:S(2)}) %collective-permute-start.4) | collective-permute-done | bytes 131104 | tf_op jit(solution)/shard_map/ppermute | solution.py:426
  20.5 2.7 %collective-permute-start.5 = (bf16[512,128]{1,0:T(8,128)(2,1)S(1)}, bf16[512,128]{1,0:T(8,128)(2,1)S(1)}, u32[]{:S(2)}, u32[]{:S(2)}) collective-permute-start(bf16[512,128]{1,0:T(8,128)(2,1)S(1)} %get-tuple-element.55), channel_id=1, source_target_pairs={{0,16},{4,20},{8,24},{12,28},{16,0},{20,4},{24,8},{28,12},{1,17},{... | collective-permute-start | bytes 393224 | tf_op jit(solution)/shard_map/ppermute | solution.py:426
  23.1 1.2 %collective-permute-start.10 = (bf16[96,2048]{1,0:T(8,128)(2,1)S(1)}, bf16[96,2048]{1,0:T(8,128)(2,1)S(1)}, u32[]{:S(2)}, u32[]{:S(2)}) collective-permute-start(bf16[96,2048]{1,0:T(8,128)(2,1)S(1)} %collective-permute-done.8.refs_1_), channel_id=1, source_target_pairs={{0,4},{4,0},{8,12},{12,8},{16,20},{20,16},{24,28},{28,24},{1,5},{5... | collective-permute-start | bytes 1179656 | tf_op jit(solution)/shard_map/ppermute | solution.py:426
  24.3 1.2 %collective-permute-done.7.refs_0_ = bf16[96,2048]{1,0:T(8,128)(2,1)S(1)} collective-permute-done((bf16[96,2048]{1,0:T(8,128)(2,1)S(1)}, bf16[96,2048]{1,0:T(8,128)(2,1)S(1)}, u32[]{:S(2)}, u32[]{:S(2)}) %collective-permute-start.7) | collective-permute-done | bytes 393248 | tf_op jit(solution)/shard_map/ppermute | solution.py:426
  25.6 3.0 %collective-permute-start.2 = (bf16[272,128]{1,0:T(8,128)(2,1)S(1)}, bf16[272,128]{1,0:T(8,128)(2,1)S(1)}, u32[]{:S(2)}, u32[]{:S(2)}) collective-permute-start(bf16[272,128]{1,0:T(8,128)(2,1)S(1)} %get-tuple-element.39), channel_id=1, source_target_pairs={{0,16},{4,20},{8,24},{12,28},{16,0},{20,4},{24,8},{28,12},{1,17},{... | collective-permute-start | bytes 208904 | tf_op jit(solution)/shard_map/ppermute | solution.py:426
  28.6 2.2 %shard_map.63.refs_1_ = f32[512,256]{1,0:T(8,128)S(1)} custom-call(bf16[512,512]{1,0:T(8,128)(2,1)S(1)} %get-tuple-element.32.q_ref, bf16[512,512]{1,0:T(8,128)(2,1)S(1)} %get-tuple-element.41.k_ref, bf16[512,512]{1,0:T(8,128)(2,1)S(1)} %get-tuple-element.33.v_ref), custom_call_target="tpu_custom_call" | custom-call | flops 268435456 | bytes 1572864 | tf_op jit(solution)/shard_map/pallas_call | solution.py:44
  30.8 2.2 %shard_map.62.refs_0_ = f32[512,256]{1,0:T(8,128)S(1)} custom-call(bf16[512,512]{1,0:T(8,128)(2,1)S(1)} %get-tuple-element.32.q_ref, bf16[512,512]{1,0:T(8,128)(2,1)S(1)} %get-tuple-element.41.k_ref, bf16[512,512]{1,0:T(8,128)(2,1)S(1)} %get-tuple-element.33.v_ref), custom_call_target="tpu_custom_call" | custom-call | flops 268435456 | bytes 1572864 | tf_op jit(solution)/shard_map/pallas_call | solution.py:44
  33.2 2.6 %shard_map.64.part_ref = f32[512,512]{1,0:T(8,128)S(1)} custom-call(bf16[512,512]{1,0:T(8,128)(2,1)S(1)} %get-tuple-element.32.q_ref, bf16[512,512]{1,0:T(8,128)(2,1)S(1)} %get-tuple-element.33.v_ref, bf16[4,128,128]{2,1,0:T(8,128)(2,1)S(1)} %get-tuple-element.53.gram_ref, f32[512,256]{1,0:T(8,128)S(1)} %shard_map.62.refs_0_, f32[512,256]{1,0:T(8,128)S(1)} %shard_map.63.refs_1_), custom_call_target="tpu_custom_call" | custom-call | flops 402653184 | bytes 2228224 | tf_op jit(solution)/shard_map/pallas_call | solution.py:44
  36.2 1.5 %collective-permute-start.6 = (bf16[2,128,512]{2,1,0:T(8,128)(2,1)S(1)}, bf16[2,128,512]{2,1,0:T(8,128)(2,1)S(1)}, u32[]{:S(2)}, u32[]{:S(2)}) collective-permute-start(bf16[2,128,512]{2,1,0:T(8,128)(2,1)S(1)} %shard_map.67), channel_id=1, source_target_pairs={{0,2},{1,3},{2,0},{3,1},{4,6},{5,7},{6,4},{7,5},{8,10},{9,11},{10,... | collective-permute-start | bytes 786440 | tf_op jit(solution)/shard_map/ppermute | solution.py:426
  38.2 0.7 %shard_map.66.own_ref = f32[2,128,2048]{2,1,0:T(8,128)S(1)} custom-call(bf16[2,128,512]{2,1,0:T(8,128)(2,1)S(1)} %shard_map.65.kept_ref, bf16[512,2048]{1,0:T(8,128)(2,1)S(1)} %copy-done), custom_call_target="tpu_custom_call" | custom-call | flops 536870912 | bytes 2359296 | tf_op jit(solution)/shard_map/pallas_call | solution.py:44
  38.9 1.7 %collective-permute-done.9.refs_2_ = bf16[96,2048]{1,0:T(8,128)(2,1)S(1)} collective-permute-done((bf16[96,2048]{1,0:T(8,128)(2,1)S(1)}, bf16[96,2048]{1,0:T(8,128)(2,1)S(1)}, u32[]{:S(2)}, u32[]{:S(2)}) %collective-permute-start.9) | collective-permute-done | bytes 393248 | tf_op jit(solution)/shard_map/ppermute | solution.py:426
  40.8 1.9 %collective-permute-done.6.came_ref = bf16[2,128,512]{2,1,0:T(8,128)(2,1)S(1)} collective-permute-done((bf16[2,128,512]{2,1,0:T(8,128)(2,1)S(1)}, bf16[2,128,512]{2,1,0:T(8,128)(2,1)S(1)}, u32[]{:S(2)}, u32[]{:S(2)}) %collective-permute-start.6) | collective-permute-done | bytes 262176 | tf_op jit(solution)/shard_map/ppermute | solution.py:426
  43.7 1.4 %collective-permute-done.12 = bf16[128,2048]{1,0:T(8,128)(2,1)S(1)} collective-permute-done((bf16[128,2048]{1,0:T(8,128)(2,1)S(1)}, bf16[128,2048]{1,0:T(8,128)(2,1)S(1)}, u32[]{:S(2)}, u32[]{:S(2)}) %collective-permute-start.12) | collective-permute-done | bytes 524320 | tf_op jit(solution)/shard_map/ppermute | solution.py:426
  45.1 0.9 %add_convert_fusion = bf16[128,2048]{1,0:T(8,128)(2,1)} fusion(f32[128,2048]{1,0:T(8,128)S(1)} %shard_map.69, bf16[128,2048]{1,0:T(8,128)(2,1)S(1)} %collective-permute-done.12), kind=kLoop, calls=%fused_computation | loop fusion | flops 786432 | bytes 2097152 | tf_op jit(solution)/shard_map/convert_element_type | solution.py:491
  (23 shorter events, 3.1 us)
Async XLA Ops:
  2.0 8.1 %collective-permute-start = (bf16[784,128]{1,0:T(8,128)(2,1)S(1)}, bf16[784,128]{1,0:T(8,128)(2,1)S(1)}, u32[]{:S(2)}, u32[]{:S(2)}) collective-permute-start(bf16[784,128]{1,0:T(8,128)(2,1)S(1)} %get-tuple-element.34), channel_id=1, source_target_pairs={{0,4},{4,0},{8,12},{12,8},{16,20},{20,16},{24,28},{28,24},{1,5},{5... | collective-permute-start | bytes 602120 | tf_op jit(solution)/shard_map/ppermute | solution.py:426
  5.1 18.1 %collective-permute-start.8 = (bf16[96,2048]{1,0:T(8,128)(2,1)S(1)}, bf16[96,2048]{1,0:T(8,128)(2,1)S(1)}, u32[]{:S(2)}, u32[]{:S(2)}) collective-permute-start(bf16[96,2048]{1,0:T(8,128)(2,1)S(1)} %get-tuple-element.57), channel_id=1, source_target_pairs={{0,2},{1,3},{2,0},{3,1},{4,6},{5,7},{6,4},{7,5},{8,10},{9,11},{10,... | collective-permute-start | bytes 1179656 | tf_op jit(solution)/shard_map/ppermute | solution.py:426
  6.6 18.9 %collective-permute-start.7 = (bf16[96,2048]{1,0:T(8,128)(2,1)S(1)}, bf16[96,2048]{1,0:T(8,128)(2,1)S(1)}, u32[]{:S(2)}, u32[]{:S(2)}) collective-permute-start(bf16[96,2048]{1,0:T(8,128)(2,1)S(1)} %get-tuple-element.56), channel_id=1, source_target_pairs={{0,2},{1,3},{2,0},{3,1},{4,6},{5,7},{6,4},{7,5},{8,10},{9,11},{10,... | collective-permute-start | bytes 1179656 | tf_op jit(solution)/shard_map/ppermute | solution.py:426
  10.0 5.0 %collective-permute-start.3 = (bf16[512,128]{1,0:T(8,128)(2,1)S(1)}, bf16[512,128]{1,0:T(8,128)(2,1)S(1)}, u32[]{:S(2)}, u32[]{:S(2)}) collective-permute-start(bf16[512,128]{1,0:T(8,128)(2,1)S(1)} %get-tuple-element.42), channel_id=1, source_target_pairs={{0,4},{4,0},{8,12},{12,8},{16,20},{20,16},{24,28},{28,24},{1,5},{5... | collective-permute-start | bytes 393224 | tf_op jit(solution)/shard_map/ppermute | solution.py:426
  10.9 7.4 %collective-permute-start.1 = (bf16[784,128]{1,0:T(8,128)(2,1)S(1)}, bf16[784,128]{1,0:T(8,128)(2,1)S(1)}, u32[]{:S(2)}, u32[]{:S(2)}) collective-permute-start(bf16[784,128]{1,0:T(8,128)(2,1)S(1)} %get-tuple-element.36), channel_id=1, source_target_pairs={{0,8},{4,12},{8,0},{12,4},{16,24},{20,28},{24,16},{28,20},{1,9},{5... | collective-permute-start | bytes 602120 | tf_op jit(solution)/shard_map/ppermute | solution.py:426
  15.2 5.0 %collective-permute-start.4 = (bf16[512,128]{1,0:T(8,128)(2,1)S(1)}, bf16[512,128]{1,0:T(8,128)(2,1)S(1)}, u32[]{:S(2)}, u32[]{:S(2)}) collective-permute-start(bf16[512,128]{1,0:T(8,128)(2,1)S(1)} %get-tuple-element.46), channel_id=1, source_target_pairs={{0,8},{4,12},{8,0},{12,4},{16,24},{20,28},{24,16},{28,20},{1,9},{5... | collective-permute-start | bytes 393224 | tf_op jit(solution)/shard_map/ppermute | solution.py:426
  16.8 22.1 %collective-permute-start.11 = (bf16[128,2048]{1,0:T(8,128)(2,1)S(1)}, bf16[128,2048]{1,0:T(8,128)(2,1)S(1)}, u32[]{:S(2)}, u32[]{:S(2)}) collective-permute-start(bf16[128,2048]{1,0:T(8,128)(2,1)S(1)} %get-tuple-element.58), channel_id=1, source_target_pairs={{0,2},{1,3},{2,0},{3,1},{4,6},{5,7},{6,4},{7,5},{8,10},{9,11},{10,... | collective-permute-start | bytes 1572872 | tf_op jit(solution)/shard_map/ppermute | solution.py:426
  20.5 15.3 %collective-permute-start.5 = (bf16[512,128]{1,0:T(8,128)(2,1)S(1)}, bf16[512,128]{1,0:T(8,128)(2,1)S(1)}, u32[]{:S(2)}, u32[]{:S(2)}) collective-permute-start(bf16[512,128]{1,0:T(8,128)(2,1)S(1)} %get-tuple-element.55), channel_id=1, source_target_pairs={{0,16},{4,20},{8,24},{12,28},{16,0},{20,4},{24,8},{28,12},{1,17},{... | collective-permute-start | bytes 393224 | tf_op jit(solution)/shard_map/ppermute | solution.py:426
  23.1 15.8 %collective-permute-start.10 = (bf16[96,2048]{1,0:T(8,128)(2,1)S(1)}, bf16[96,2048]{1,0:T(8,128)(2,1)S(1)}, u32[]{:S(2)}, u32[]{:S(2)}) collective-permute-start(bf16[96,2048]{1,0:T(8,128)(2,1)S(1)} %collective-permute-done.8.refs_1_), channel_id=1, source_target_pairs={{0,4},{4,0},{8,12},{12,8},{16,20},{20,16},{24,28},{28,24},{1,5},{5... | collective-permute-start | bytes 1179656 | tf_op jit(solution)/shard_map/ppermute | solution.py:426
  25.5 15.2 %collective-permute-start.9 = (bf16[96,2048]{1,0:T(8,128)(2,1)S(1)}, bf16[96,2048]{1,0:T(8,128)(2,1)S(1)}, u32[]{:S(2)}, u32[]{:S(2)}) collective-permute-start(bf16[96,2048]{1,0:T(8,128)(2,1)S(1)} %collective-permute-done.7.refs_0_), channel_id=1, source_target_pairs={{0,4},{4,0},{8,12},{12,8},{16,20},{20,16},{24,28},{28,24},{1,5},{5... | collective-permute-start | bytes 1179656 | tf_op jit(solution)/shard_map/ppermute | solution.py:426
  25.6 7.4 %collective-permute-start.2 = (bf16[272,128]{1,0:T(8,128)(2,1)S(1)}, bf16[272,128]{1,0:T(8,128)(2,1)S(1)}, u32[]{:S(2)}, u32[]{:S(2)}) collective-permute-start(bf16[272,128]{1,0:T(8,128)(2,1)S(1)} %get-tuple-element.39), channel_id=1, source_target_pairs={{0,16},{4,20},{8,24},{12,28},{16,0},{20,4},{24,8},{28,12},{1,17},{... | collective-permute-start | bytes 208904 | tf_op jit(solution)/shard_map/ppermute | solution.py:426
  32.9 2.9 %copy-start.1 = (f32[512]{0:T(512)S(1)}, f32[512]{0:T(512)}, u32[]{:S(2)}) copy-start(f32[512]{0:T(512)} %param.8) | copy-start | bytes 6148
  35.8 2.4 %copy-start = (bf16[512,2048]{1,0:T(8,128)(2,1)S(1)}, bf16[512,2048]{1,0:T(8,128)(2,1)}, u32[]{:S(2)}) copy-start(bf16[512,2048]{1,0:T(8,128)(2,1)} %w_ref.1) | copy-start | bytes 6291460
  36.2 6.4 %collective-permute-start.6 = (bf16[2,128,512]{2,1,0:T(8,128)(2,1)S(1)}, bf16[2,128,512]{2,1,0:T(8,128)(2,1)S(1)}, u32[]{:S(2)}, u32[]{:S(2)}) collective-permute-start(bf16[2,128,512]{2,1,0:T(8,128)(2,1)S(1)} %shard_map.67), channel_id=1, source_target_pairs={{0,2},{1,3},{2,0},{3,1},{4,6},{5,7},{6,4},{7,5},{8,10},{9,11},{10,... | collective-permute-start | bytes 786440 | tf_op jit(solution)/shard_map/ppermute | solution.py:426
  43.1 2.0 %collective-permute-start.12 = (bf16[128,2048]{1,0:T(8,128)(2,1)S(1)}, bf16[128,2048]{1,0:T(8,128)(2,1)S(1)}, u32[]{:S(2)}, u32[]{:S(2)}) collective-permute-start(bf16[128,2048]{1,0:T(8,128)(2,1)S(1)} %shard_map.70), channel_id=1, source_target_pairs={{0,1},{1,0},{2,3},{3,2},{4,5},{5,4},{6,7},{7,6},{8,9},{9,8},{10,11... | collective-permute-start | bytes 1572872 | tf_op jit(solution)/shard_map/ppermute | solution.py:426
where the time goes:
time: 46.2 us; the launch traced here: 46 us
  starting transfers between devices  18.9 us (41%)
  Pallas kernels  16.1 us (35%)
  waiting for transfers between devices  9.93 us (21%)
  other arithmetic  0.9 us (2%)
    ppermute x13, starting transfers between devices, flip(): return lax.ppermute(value, axis, [(i, i ^ bit) for i in range(count)])  18.9 us
    pallas_call x16, Pallas kernels, call(): pl.pallas_call(kernel, in_specs=[pl.BlockSpec(memory_space=space) for a,...  16.1 us
    ppermute x13, waiting for transfers between devices, flip(): return lax.ppermute(value, axis, [(i, i ^ bit) for i in range(count)])  9.93 us
  transfers between devices with their start and end apart: 13, of which 6 were waited for; matrix products, arithmetic and copies ran while one was open for 0% of the time, Pallas kernels for 30%

commit v1 on v0

v1 whole, which is shorter than its diff:
```python
import functools

import jax
import jax.numpy as jnp
from jax import lax
from jax.experimental import pallas as pl
from jax.experimental.pallas import tpu as pltpu
from jax.sharding import PartitionSpec as P


DH = 128
DIAG = 16
SHARES = (5, 5, 4)
F32 = jnp.float32
BF16 = jnp.bfloat16


def mm(a, b):
    return lax.dot_general(a, b, (((1,), (0,)), ((), ())), preferred_element_type=F32)


def mm_nt(a, b):
    return lax.dot_general(a, b, (((1,), (1,)), ((), ())), preferred_element_type=F32)


def mm_tn(a, b):
    return lax.dot_general(a, b, (((0,), (0,)), ((), ())), preferred_element_type=F32)


def row_col(n):
    return lax.broadcasted_iota(jnp.int32, (n, n), 0), lax.broadcasted_iota(jnp.int32, (n, n), 1)


def is_upper(bit):
    return lax.bitwise_and(lax.axis_index("seq"), bit) != 0


def columns(h):
    return slice(h * DH, (h + 1) * DH)


def call(kernel, ins, outs, flops=0, scratch=(), mib=4):
    arrays = [pltpu.with_memory_space_constraint(a, space) if space is pltpu.HBM else a for a, space in ins]
    data = sum(a.size * a.dtype.itemsize for a in arrays)
    return pl.pallas_call(
        kernel,
        in_specs=[pl.BlockSpec(memory_space=space) for a, space in ins],
        out_specs=[pl.BlockSpec(memory_space=pltpu.VMEM) for o in outs],
        out_shape=[pltpu.VMEM(shape, dtype) for shape, dtype in outs],
        scratch_shapes=list(scratch),
        compiler_params=pltpu.CompilerParams(vmem_limit_bytes=mib << 20),
        cost_estimate=pl.CostEstimate(flops=int(flops), bytes_accessed=int(data), transcendentals=0),
    )(*arrays)


def vm(*arrays):
    return [(a, pltpu.VMEM) for a in arrays]


def pack(grams):
    heads = len(grams)
    row, col = row_col(DH)
    parts, diagonals = [], []
    for p in range(0, heads, 2):
        a, b = grams[p], grams[min(p + 1, heads - 1)]
        parts.append(jnp.where(row <= col, a, b))
        diagonals.append(jnp.sum(jnp.where(row == col, b, 0.0), axis=0, keepdims=True))
    diagonals += [jnp.zeros((1, DH), F32)] * (DIAG - len(diagonals))
    return parts, jnp.concatenate(diagonals, axis=0)


def unpack(rows_of, heads):
    pairs = (heads + 1) // 2
    row, col = row_col(DH)
    diagonals = rows_of(pairs * DH, DIAG)
    grams = []
    for p in range(pairs):
        m = rows_of(p * DH, DH)
        t = m.T
        d = jnp.broadcast_to(diagonals[p : p + 1, :], (DH, DH))
        grams.append(jnp.where(row <= col, m, t))
        grams.append(jnp.where(row > col, m, jnp.where(row < col, t, d)))
    return grams[:heads]


def packed_rows(heads):
    return (heads + 1) // 2 * DH + DIAG


def sums_kernel(chunks, q_hbm, k_hbm, v_hbm, w_hbm, q_ref, k_ref, v_ref, own_ref, send_ref, *refs):
    *w_refs, sem, w_sem = refs
    rows, width = q_ref.shape
    heads = width // DH
    size = rows // chunks
    copies = []
    for c in range(chunks):
        at = pl.ds(c * size, size)
        for n, (src, dst) in enumerate(((k_hbm, k_ref), (q_hbm, q_ref), (v_hbm, v_ref))):
            copies.append(pltpu.make_async_copy(src.at[at], dst.at[at], sem.at[c, n]))
    sizes = [ref.shape[0] for ref in w_refs]
    first = lax.bitwise_and(lax.axis_index("seq"), 1) * sum(sizes)
    for n, w_ref in enumerate(w_refs):
        at = pl.multiple_of(first + sum(sizes[:n]), 16)
        copies.append(pltpu.make_async_copy(w_hbm.at[pl.ds(at, sizes[n])], w_ref, w_sem.at[n]))
    for copy in copies:
        copy.start()
    grams = [None] * heads
    crosses = [None] * heads
    for c in range(chunks):
        at = pl.ds(c * size, size)
        copies[3 * c].wait()
        for h in range(heads):
            k = k_ref[at, columns(h)]
            gram = mm_tn(k, k)
            grams[h] = gram if c == 0 else grams[h] + gram
        copies[3 * c + 1].wait()
        copies[3 * c + 2].wait()
        for h in range(heads):
            cross = mm_tn(q_ref[at, columns(h)], v_ref[at, columns(h)])
            crosses[h] = cross if c == 0 else crosses[h] + cross
    parts, diagonals = pack(grams)
    base = packed_rows(heads)
    places = [(p * DH, part) for p, part in enumerate(parts)] + [(base - DIAG, diagonals)]
    for at, part in places + [(base + h * DH, cross) for h, cross in enumerate(crosses)]:
        own_ref[pl.ds(at, part.shape[0]), :] = part
        send_ref[pl.ds(at, part.shape[0]), :] = part.astype(BF16)
    for copy in copies[3 * chunks :]:
        copy.wait()


def local_sums(q, k, v, weight, sizes):
    rows, width = q.shape
    heads = width // DH
    chunks = 2 if rows % 32 == 0 else 1
    return call(
        functools.partial(sums_kernel, chunks),
        [(a, pltpu.HBM) for a in (q, k, v, weight)],
        [((rows, width), BF16)] * 3
        + [((packed_rows(heads) + heads * DH, DH), dtype) for dtype in (F32, BF16)]
        + [((size, weight.shape[1]), BF16) for size in sizes],
        flops=4 * rows * width * DH,
        scratch=[pltpu.SemaphoreType.DMA((chunks, 3)), pltpu.SemaphoreType.DMA((len(sizes),))],
        mib=6,
    )


def pairs_kernel(block, q_ref, k_ref, v_ref, w_hbm, own_ref, send_ref, paired_ref, w_ref, w_sem):
    rest = w_ref.shape[0]
    copy = pltpu.make_async_copy(w_hbm.at[pl.ds(w_hbm.shape[0] - rest, rest)], w_ref, w_sem)
    copy.start()
    rows, width = q_ref.shape
    for h in range(width // DH):
        pair = None
        for start in range(0, rows, block):
            span = rows - start
            at, on = pl.ds(start, block), pl.ds(start, span)
            k = k_ref[at, columns(h)]
            row = lax.broadcasted_iota(jnp.int32, (block, span), 0)
            col = lax.broadcasted_iota(jnp.int32, (block, span), 1)
            paired = jnp.where(row < col, mm_nt(k, q_ref[on, columns(h)]), 0.0).astype(BF16)
            paired_ref[h, at, start:rows] = paired
            here = mm_tn(k, mm(paired, v_ref[on, columns(h)]).astype(BF16))
            pair = pair + here if start else here
        own_ref[h] = pair
        send_ref[pl.ds(h * DH, DH), :] = pair.astype(BF16)
    copy.wait()


def local_pairs(q, k, v, weight, rest, block):
    rows, width = q.shape
    heads = width // DH
    return call(
        functools.partial(pairs_kernel, block),
        vm(q, k, v) + [(weight, pltpu.HBM)],
        [
            ((heads, DH, DH), F32),
            ((heads * DH, DH), BF16),
            ((heads, rows, rows), BF16),
            ((rest, weight.shape[1]), BF16),
        ],
        flops=4 * rows * width * block,
        scratch=[pltpu.SemaphoreType.DMA],
        mib=8,
    )


def union_sums_kernel(bit, first, last, got_ref, own_ref, *refs):
    refs = list(refs)
    ahead_ref = None if first else refs.pop(0)
    ahead_out, send_ref = refs[:2]
    got = got_ref[...].astype(F32)
    total = own_ref[...] + got
    sent = send_ref.shape[0]
    send_ref[...] = total[:sent].astype(BF16)
    if not last:
        refs[2][...] = total
    ahead = is_upper(bit).astype(F32) * got
    ahead_out[...] = ahead if first else ahead_ref[...] + ahead


def union_sums(bit, got, own, ahead, heads, last):
    first = ahead is None
    sent = packed_rows(heads) if last else got.shape[0]
    return call(
        functools.partial(union_sums_kernel, bit, first, last),
        vm(got, own) + ([] if first else vm(ahead)),
        [(own.shape, F32), ((sent, DH), BF16)] + ([] if last else [(own.shape, F32)]),
    )


def union_pairs_kernel(bit, first, last, got_ref, own_ref, sums_got_ref, sums_ref, *refs):
    refs = list(refs)
    if not first:
        before_ref, ahead_ref = refs[:2]
        refs = refs[2:]
    before_out, send_ref = refs[:2]
    heads = own_ref.shape[0]
    base = packed_rows(heads)
    upper = is_upper(bit)
    weight = upper.astype(F32)

    def came_rows(at, count):
        return sums_got_ref[pl.ds(at, count), :].astype(F32)

    def left_rows(at, count):
        return jnp.where(upper, came_rows(at, count), sums_ref[pl.ds(at, count), :])

    lefts = unpack(left_rows, heads)
    cames = None if first else unpack(came_rows, heads)
    for h in range(heads):
        at = pl.ds(base + h * DH, DH)
        right = jnp.where(upper, sums_ref[at, :], sums_got_ref[at, :].astype(F32))
        got = got_ref[pl.ds(h * DH, DH), :].astype(F32)
        total = own_ref[h] + got + mm(lefts[h].astype(BF16), right.astype(BF16))
        if not last:
            refs[2][h] = total
        send_ref[pl.ds(h * DH, DH), :] = total.astype(BF16)
        if first:
            before_out[h] = weight * got
        else:
            product = mm(cames[h].astype(BF16), ahead_ref[at, :].astype(BF16))
            before_out[h] = before_ref[h] + weight * (got + product)


def union_pairs(bit, got, own, sums_got, sums, before, ahead, last):
    first = before is None
    return call(
        functools.partial(union_pairs_kernel, bit, first, last),
        vm(got, own, sums_got, sums) + ([] if first else vm(before, ahead)),
        [(own.shape, F32), (got.shape, BF16)] + ([] if last else [(own.shape, F32)]),
        flops=own.size * 4 * DH,
    )


def ahead_kernel(bit, got_ref, ahead_ref, before_ref, gram_ref, base_ref):
    weight = is_upper(bit).astype(F32)
    heads = before_ref.shape[0]
    base = packed_rows(heads)

    def came_rows(at, count):
        return got_ref[pl.ds(at, count), :].astype(F32)

    def ahead_rows(at, count):
        return ahead_ref[pl.ds(at, count), :] + weight * came_rows(at, count)

    cames = unpack(came_rows, heads)
    for h, gram in enumerate(unpack(ahead_rows, heads)):
        gram_ref[h] = gram.astype(BF16)
        cross = ahead_ref[pl.ds(base + h * DH, DH), :]
        base_ref[h] = before_ref[h] + weight * mm(cames[h].astype(BF16), cross.astype(BF16))


def ahead_of_device(bit, got, ahead, before):
    return call(
        functools.partial(ahead_kernel, bit),
        vm(got, ahead, before),
        [(before.shape, BF16), (before.shape, F32)],
        flops=before.size * 2 * DH,
    )


def inner_kernel(block, heads, q_ref, k_ref, v_ref, paired_ref, out_ref):
    rows = q_ref.shape[0]
    row, col = row_col(block)
    for n, h in enumerate(heads):
        for start in range(0, rows, block):
            at, end = pl.ds(start, block), start + block
            scores = mm_nt(q_ref[at, columns(h)], k_ref[pl.ds(0, end), columns(h)]).astype(BF16)
            result = None
            for first in range(0, end, block):
                upto = first + block
                mixing = mm(scores[:, :upto], paired_ref[h, pl.ds(0, upto), first:upto])
                if first == start:
                    mixing = jnp.where(row >= col, mixing, 0.0)
                more = mm(mixing.astype(BF16), v_ref[pl.ds(first, block), columns(h)])
                result = result + more if first else more
            out_ref[at, columns(n)] = result


def inner(q, k, v, paired, block, heads):
    rows = q.shape[0]
    return call(
        functools.partial(inner_kernel, block, heads),
        vm(q, k, v, paired),
        [((rows, len(heads) * DH), F32)],
        flops=rows * len(heads) * DH * 8 * block,
    )[0]


def outer_kernel(block, q_ref, v_ref, gram_ref, *refs):
    *part_refs, out_ref = refs
    rows = q_ref.shape[0]
    parts = [(ref, n) for ref in part_refs for n in range(ref.shape[1] // DH)]
    for h, (part_ref, n) in enumerate(parts):
        state = mm(q_ref[:, columns(h)], gram_ref[h]).astype(BF16)
        for start in range(0, rows, block):
            at, end = pl.ds(start, block), start + block
            row = lax.broadcasted_iota(jnp.int32, (block, end), 0) + start
            col = lax.broadcasted_iota(jnp.int32, (block, end), 1)
            mixing = mm_nt(state[start:end], q_ref[pl.ds(0, end), columns(h)])
            mixing = jnp.where(row >= col, mixing, 0.0).astype(BF16)
            out_ref[at, columns(h)] = part_ref[at, columns(n)] + mm(mixing, v_ref[pl.ds(0, end), columns(h)])


def outer(q, v, gram, parts, block):
    rows, width = q.shape
    return call(
        functools.partial(outer_kernel, block),
        vm(q, v, gram, *parts),
        [((rows, width), F32)],
        flops=rows * width * 6 * block,
    )[0]


def normed_kernel(bit, blocks, other, q_ref, part_ref, base_ref, got_ref, gain_ref, out_ref):
    weight = is_upper(bit).astype(F32)
    size = q_ref.shape[0] // blocks
    first = lax.bitwise_xor(lax.axis_index("head"), other)
    for h in range(base_ref.shape[0]):
        pair = (base_ref[h] + weight * got_ref[pl.ds(h * DH, DH), :].astype(F32)).astype(BF16)
        for j in range(blocks // 2):
            at = pl.ds(pl.multiple_of(lax.bitwise_xor(first, j) * size, size), size)
            attended = part_ref[at, columns(h)] + mm(q_ref[at, columns(h)], pair)
            mean = jnp.mean(attended * attended, axis=-1, keepdims=True)
            normed = attended * lax.rsqrt(mean + 1e-6) * gain_ref[:, columns(h)]
            out_ref[j, :, columns(h)] = normed.astype(BF16)


def normed_blocks(bit, other, q, part, base, got, gain, blocks):
    rows, width = q.shape
    return call(
        functools.partial(normed_kernel, bit, blocks, other),
        vm(q, part, base, got, gain),
        [((blocks // 2, rows // blocks, width), BF16)],
        flops=rows * width * DH,
    )[0]


def weights_kernel(shares, *refs):
    *parts, rest_ref, out_ref = refs
    sizes = [ref.shape[0] for ref in parts[:shares]]
    odd = lax.bitwise_and(lax.axis_index("seq"), 1)
    for n, size in enumerate(sizes):
        for first, ref in ((odd, parts[n]), (1 - odd, parts[shares + n])):
            at = pl.multiple_of(first * sum(sizes) + sum(sizes[:n]), 16)
            out_ref[pl.ds(at, size), :] = ref[...]
    out_ref[pl.ds(2 * sum(sizes), rest_ref.shape[0]), :] = rest_ref[...]


def join_weights(direct, neighbour, rest):
    rows = sum(part.shape[0] for part in (*direct, *neighbour, rest))
    return call(
        functools.partial(weights_kernel, len(direct)),
        vm(*direct, *neighbour, rest),
        [((rows, rest.shape[1]), BF16)],
        mib=8,
    )[0]


def project_own_kernel(kept_ref, w_ref, out_ref):
    blocks, size, width = kept_ref.shape
    kept = kept_ref[...].reshape(blocks * size, width)
    span = out_ref.shape[2]
    tile = 512 if span % 512 == 0 else span
    for start in range(0, span, tile):
        at = slice(start, start + tile)
        out_ref[:, :, at] = mm(kept, w_ref[:, at]).reshape(blocks, size, tile)


def project_own(kept, weight):
    blocks, size, width = kept.shape
    span = weight.shape[1]
    return call(
        project_own_kernel,
        vm(kept, weight),
        [((blocks, size, span), F32)],
        flops=2 * blocks * size * width * span,
        mib=8,
    )[0]


def project_kernel(index, own_ref, came_ref, w_ref, out_ref):
    span = out_ref.shape[1]
    tile = 512 if span % 512 == 0 else span
    for start in range(0, span, tile):
        at = slice(start, start + tile)
        out_ref[:, at] = (own_ref[index, :, at] + mm(came_ref[index], w_ref[:, at])).astype(out_ref.dtype)


def project(index, own, came, weight, dtype):
    _, size, span = own.shape
    return call(
        functools.partial(project_kernel, index),
        vm(own, came, weight),
        [((size, span), dtype)],
        flops=2 * size * came.shape[2] * span,
        mib=8,
    )[0]


def flip(value, axis, bit):
    count = lax.axis_size(axis)
    return lax.ppermute(value, axis, [(i, i ^ bit) for i in range(count)])


def shards(queries, key_vectors, value_vectors, norm_gain, out_weight):
    rows, width = queries.shape
    seq_count, head_count = lax.axis_size("seq"), lax.axis_size("head")
    block = 256 if rows % 256 == 0 else rows

    top = head_count // 2
    features = out_weight.shape[0]
    sizes = [features * n // 32 // 16 * 16 for n in SHARES]

    q, k, v, sums, sums_send, *weight_shares = local_sums(
        queries, key_vectors, value_vectors, out_weight, sizes
    )
    pairs, pairs_send, paired, weight_rest = local_pairs(
        q, k, v, out_weight, features - 2 * sum(sizes), block
    )
    direct = [flip(w, "head", top) for w in weight_shares]
    neighbour = [flip(w, "seq", 1) for w in direct]
    rest = flip(weight_rest, "head", top)
    heads = width // DH
    parts = [
        inner(q, k, v, paired, block, tuple(range(at, min(at + (heads + 1) // 2, heads))))
        for at in range(0, heads, (heads + 1) // 2)
    ]
    ahead = before = None
    bit = 1
    while 2 * bit < seq_count:
        sums_got = flip(sums_send, "seq", bit)
        pairs_got = flip(pairs_send, "seq", bit)
        last = 4 * bit >= seq_count
        old = ahead
        ahead, sums_send, *more_sums = union_sums(bit, sums_got, sums, ahead, heads, last)
        before, pairs_send, *more_pairs = union_pairs(
            bit, pairs_got, pairs, sums_got, sums, before, old, last
        )
        if not last:
            (pairs,), (sums,) = more_pairs, more_sums
        bit *= 2
    gram_got = flip(sums_send, "seq", bit)
    pairs_got = flip(pairs_send, "seq", bit)
    gram, base = ahead_of_device(bit, gram_got, ahead, before)
    part = outer(q, v, gram, parts, block)

    gain = norm_gain.reshape(1, width)
    sent = normed_blocks(bit, top, q, part, base, pairs_got, gain, head_count)
    came = flip(sent, "head", top)
    kept = normed_blocks(bit, 0, q, part, base, pairs_got, gain, head_count)
    own = project_own(kept, out_weight)
    weight_came = join_weights(direct, neighbour, rest)

    count = top
    if count == 1:
        return project(0, own, came, weight_came, BF16)
    results = {
        j: project(j, own, came, weight_came, BF16 if 2 * j >= count else F32) for j in reversed(range(count))
    }
    while count > 1:
        count //= 2
        for j in range(count):
            got = flip(results[count + j].astype(BF16), "head", count)
            results[j] = results[j].astype(F32) + got.astype(F32)
    return results[0].astype(BF16)


def solution(mesh):
    in_specs = (P("seq", "head"), P("seq", "head"), P("seq", "head"), P("head"), P("head", None))
    out_specs = P(("seq", "head"), None)

    return jax.shard_map(shards, mesh=mesh, in_specs=in_specs, out_specs=out_specs, check_vma=False)
```

time: 46.2 us -> 48.5 us (1.050)
  waiting for transfers between devices: 9.93 us -> 15.7 us
  Pallas kernels: 16.1 us -> 12.4 us
    ppermute x13 -> x15, waiting for transfers between devices: 9.93 us -> 15.7 us  [flip(): return lax.ppermute(value, axis, [(i, i ^ bit) for i in range(count)])]
    pallas_call x16, Pallas kernels: 16.1 us -> 12.4 us  [call(): pl.pallas_call(kernel, in_specs=[pl.BlockSpec(memory_space=space) for a,...]
    ppermute x13 -> x15, starting transfers between devices: 18.9 us -> 19.2 us  [flip(): return lax.ppermute(value, axis, [(i, i ^ bit) for i in range(count)])]
  transfers between devices with their start and end apart: 13 -> 15, of which waited for: 6 -> 6; matrix products, arithmetic and copies ran while one was open for 0% -> 0% of each run, Pallas kernels for 30% -> 21%
where the time goes in v1:
time: 48.5 us; the launch traced here: 48.4 us
  starting transfers between devices  19.2 us (40%)
  waiting for transfers between devices  15.7 us (32%)
  Pallas kernels  12.4 us (26%)
  other arithmetic  0.9 us (2%)
    ppermute x15, starting transfers between devices, flip(): return lax.ppermute(value, axis, [(i, i ^ bit) for i in range(count)])  19.2 us
    ppermute x15, waiting for transfers between devices, flip(): return lax.ppermute(value, axis, [(i, i ^ bit) for i in range(count)])  15.7 us
    pallas_call x16, Pallas kernels, call(): pl.pallas_call(kernel, in_specs=[pl.BlockSpec(memory_space=space) for a,...  12.4 us
  transfers between devices with their start and end apart: 15, of which 6 were waited for; matrix products, arithmetic and copies ran while one was open for 0% of the time, Pallas kernels for 21%

profile of v1, /device:TPU:0, one launch (start us, length us, event | category | flops | bytes accessed | tf_op | source)
XLA Modules:
  0.0 48.4 jit_solution(17884376230466711474)
XLA Ops:
  0.0 2.0 %shard_map.55 = (bf16[512,512]{1,0:T(8,128)(2,1)S(1)}, bf16[512,512]{1,0:T(8,128)(2,1)S(1)}, bf16[512,512]{1,0:T(8,128)(2,1)S(1)}, f32[784,128]{1,0:T(8,128)S(1)...) custom-call(bf16[512,512]{1,0:T(8,128)(2,1)} %q_hbm.1, ...), custom_call_target="tpu_custom_call" | custom-call | flops 134217728 | bytes 3670016 | tf_op jit(solution)/shard_map/pallas_call | solution.py:45
  2.0 3.1 %collective-permute-start = (bf16[784,128]{1,0:T(8,128)(2,1)S(1)}, bf16[784,128]{1,0:T(8,128)(2,1)S(1)}, u32[]{:S(2)}, u32[]{:S(2)}) collective-permute-start(bf16[784,128]{1,0:T(8,128)(2,1)S(1)} %get-tuple-element.31), channel_id=1, source_target_pairs={{0,4},{4,0},{8,12},{12,8},{16,20},{20,16},{24,28},{28,24},{1,5},{5... | collective-permute-start | bytes 602120 | tf_op jit(solution)/shard_map/ppermute | solution.py:423
  5.1 2.3 %shard_map.58 = (f32[4,128,128]{2,1,0:T(8,128)S(1)}, bf16[512,128]{1,0:T(8,128)(2,1)S(1)}, bf16[4,512,512]{2,1,0:T(8,128)(2,1)S(1)}, bf16[64,2048]{1,0:T(8,128)(2,1)S(1)}) custom-call(bf16[512,512]{1,0:T(8,128)(2,1)S(1)} %get-tuple-element.29.q_ref, bf16[512,512]{1,0:T(8,128)(2,1)S(1)} %get-tuple-element.38.k_ref, ...), custom_call_target="tpu_custom_call" | custom-call | flops 268435456 | bytes 3670016 | tf_op jit(solution)/shard_map/pallas_call | solution.py:45
  7.5 2.0 %collective-permute-start.7 = (bf16[80,2048]{1,0:T(8,128)(2,1)S(1)}, bf16[80,2048]{1,0:T(8,128)(2,1)S(1)}, u32[]{:S(2)}, u32[]{:S(2)}) collective-permute-start(bf16[80,2048]{1,0:T(8,128)(2,1)S(1)} %get-tuple-element.49), channel_id=1, source_target_pairs={{0,2},{1,3},{2,0},{3,1},{4,6},{5,7},{6,4},{7,5},{8,10},{9,11},{10,... | collective-permute-start | bytes 983048 | tf_op jit(solution)/shard_map/ppermute | solution.py:423
  9.5 1.0 %collective-permute-done.got_ref.sums_got_ref = bf16[784,128]{1,0:T(8,128)(2,1)S(1)} collective-permute-done((bf16[784,128]{1,0:T(8,128)(2,1)S(1)}, bf16[784,128]{1,0:T(8,128)(2,1)S(1)}, u32[]{:S(2)}, u32[]{:S(2)}) %collective-permute-start) | collective-permute-done | bytes 200736 | tf_op jit(solution)/shard_map/ppermute | solution.py:423
  10.6 2.1 %collective-permute-start.1 = (bf16[784,128]{1,0:T(8,128)(2,1)S(1)}, bf16[784,128]{1,0:T(8,128)(2,1)S(1)}, u32[]{:S(2)}, u32[]{:S(2)}) collective-permute-start(bf16[784,128]{1,0:T(8,128)(2,1)S(1)} %get-tuple-element.33), channel_id=1, source_target_pairs={{0,8},{4,12},{8,0},{12,4},{16,24},{20,28},{24,16},{28,20},{1,9},{5... | collective-permute-start | bytes 602120 | tf_op jit(solution)/shard_map/ppermute | solution.py:423
  12.7 1.5 %collective-permute-start.9 = (bf16[64,2048]{1,0:T(8,128)(2,1)S(1)}, bf16[64,2048]{1,0:T(8,128)(2,1)S(1)}, u32[]{:S(2)}, u32[]{:S(2)}) collective-permute-start(bf16[64,2048]{1,0:T(8,128)(2,1)S(1)} %get-tuple-element.51), channel_id=1, source_target_pairs={{0,2},{1,3},{2,0},{3,1},{4,6},{5,7},{6,4},{7,5},{8,10},{9,11},{10,... | collective-permute-start | bytes 786440 | tf_op jit(solution)/shard_map/ppermute | solution.py:423
  14.4 0.6 %collective-permute-start.4 = (bf16[512,128]{1,0:T(8,128)(2,1)S(1)}, bf16[512,128]{1,0:T(8,128)(2,1)S(1)}, u32[]{:S(2)}, u32[]{:S(2)}) collective-permute-start(bf16[512,128]{1,0:T(8,128)(2,1)S(1)} %get-tuple-element.41), channel_id=1, source_target_pairs={{0,8},{4,12},{8,0},{12,4},{16,24},{20,28},{24,16},{28,20},{1,9},{5... | collective-permute-start | bytes 393224 | tf_op jit(solution)/shard_map/ppermute | solution.py:423
  15.0 4.5 %collective-permute-done.4.got_ref = bf16[512,128]{1,0:T(8,128)(2,1)S(1)} collective-permute-done((bf16[512,128]{1,0:T(8,128)(2,1)S(1)}, bf16[512,128]{1,0:T(8,128)(2,1)S(1)}, u32[]{:S(2)}, u32[]{:S(2)}) %collective-permute-start.4) | collective-permute-done | bytes 131104 | tf_op jit(solution)/shard_map/ppermute | solution.py:423
  19.8 2.8 %collective-permute-start.5 = (bf16[512,128]{1,0:T(8,128)(2,1)S(1)}, bf16[512,128]{1,0:T(8,128)(2,1)S(1)}, u32[]{:S(2)}, u32[]{:S(2)}) collective-permute-start(bf16[512,128]{1,0:T(8,128)(2,1)S(1)} %get-tuple-element.48), channel_id=1, source_target_pairs={{0,16},{4,20},{8,24},{12,28},{16,0},{20,4},{24,8},{28,12},{1,17},{... | collective-permute-start | bytes 393224 | tf_op jit(solution)/shard_map/ppermute | solution.py:423
  22.9 1.4 %shard_map.62.refs_0_ = f32[512,256]{1,0:T(8,128)S(1)} custom-call(bf16[512,512]{1,0:T(8,128)(2,1)S(1)} %get-tuple-element.29.q_ref, bf16[512,512]{1,0:T(8,128)(2,1)S(1)} %get-tuple-element.38.k_ref, bf16[512,512]{1,0:T(8,128)(2,1)S(1)} %get-tuple-element.30.v_ref, bf16[4,512,512]{2,1,0:T(8,128)(2,1)S(1)} %get-tuple-element.46.paired_ref), custom_call_target="tpu_custom_call" | custom-call | flops 268435456 | bytes 3670016 | tf_op jit(solution)/shard_map/pallas_call | solution.py:45
  24.3 2.1 %collective-permute-start.10 = (bf16[80,2048]{1,0:T(8,128)(2,1)S(1)}, bf16[80,2048]{1,0:T(8,128)(2,1)S(1)}, u32[]{:S(2)}, u32[]{:S(2)}) collective-permute-start(bf16[80,2048]{1,0:T(8,128)(2,1)S(1)} %collective-permute-done.7.refs_0_), channel_id=1, source_target_pairs={{0,4},{4,0},{8,12},{12,8},{16,20},{20,16},{24,28},{28,24},{1,5},{5... | collective-permute-start | bytes 983048 | tf_op jit(solution)/shard_map/ppermute | solution.py:423
  26.4 0.7 %collective-permute-start.11 = (bf16[80,2048]{1,0:T(8,128)(2,1)S(1)}, bf16[80,2048]{1,0:T(8,128)(2,1)S(1)}, u32[]{:S(2)}, u32[]{:S(2)}) collective-permute-start(bf16[80,2048]{1,0:T(8,128)(2,1)S(1)} %collective-permute-done.8.refs_1_), channel_id=1, source_target_pairs={{0,4},{4,0},{8,12},{12,8},{16,20},{20,16},{24,28},{28,24},{1,5},{5... | collective-permute-start | bytes 983048 | tf_op jit(solution)/shard_map/ppermute | solution.py:423
  27.1 1.4 %shard_map.63.refs_1_ = f32[512,256]{1,0:T(8,128)S(1)} custom-call(bf16[512,512]{1,0:T(8,128)(2,1)S(1)} %get-tuple-element.29.q_ref, bf16[512,512]{1,0:T(8,128)(2,1)S(1)} %get-tuple-element.38.k_ref, bf16[512,512]{1,0:T(8,128)(2,1)S(1)} %get-tuple-element.30.v_ref, bf16[4,512,512]{2,1,0:T(8,128)(2,1)S(1)} %get-tuple-element.46.paired_ref), custom_call_target="tpu_custom_call" | custom-call | flops 268435456 | bytes 3670016 | tf_op jit(solution)/shard_map/pallas_call | solution.py:45
  28.5 0.8 %collective-permute-done.9.refs_2_ = bf16[64,2048]{1,0:T(8,128)(2,1)S(1)} collective-permute-done((bf16[64,2048]{1,0:T(8,128)(2,1)S(1)}, bf16[64,2048]{1,0:T(8,128)(2,1)S(1)}, u32[]{:S(2)}, u32[]{:S(2)}) %collective-permute-start.9) | collective-permute-done | bytes 262176 | tf_op jit(solution)/shard_map/ppermute | solution.py:423
  29.3 1.6 %collective-permute-start.13 = (bf16[64,2048]{1,0:T(8,128)(2,1)S(1)}, bf16[64,2048]{1,0:T(8,128)(2,1)S(1)}, u32[]{:S(2)}, u32[]{:S(2)}) collective-permute-start(bf16[64,2048]{1,0:T(8,128)(2,1)S(1)} %get-tuple-element.52), channel_id=1, source_target_pairs={{0,2},{1,3},{2,0},{3,1},{4,6},{5,7},{6,4},{7,5},{8,10},{9,11},{10,... | collective-permute-start | bytes 786440 | tf_op jit(solution)/shard_map/ppermute | solution.py:423
  31.0 1.5 %collective-permute-start.12 = (bf16[64,2048]{1,0:T(8,128)(2,1)S(1)}, bf16[64,2048]{1,0:T(8,128)(2,1)S(1)}, u32[]{:S(2)}, u32[]{:S(2)}) collective-permute-start(bf16[64,2048]{1,0:T(8,128)(2,1)S(1)} %collective-permute-done.9.refs_2_), channel_id=1, source_target_pairs={{0,4},{4,0},{8,12},{12,8},{16,20},{20,16},{24,28},{28,24},{1,5},{5... | collective-permute-start | bytes 786440 | tf_op jit(solution)/shard_map/ppermute | solution.py:423
  32.7 1.8 %shard_map.64.part_ref = f32[512,512]{1,0:T(8,128)S(1)} custom-call(bf16[512,512]{1,0:T(8,128)(2,1)S(1)} %get-tuple-element.29.q_ref, bf16[512,512]{1,0:T(8,128)(2,1)S(1)} %get-tuple-element.30.v_ref, bf16[4,128,128]{2,1,0:T(8,128)(2,1)S(1)} %get-tuple-element.45.gram_ref, f32[512,256]{1,0:T(8,128)S(1)} %shard_map.62.refs_0_, f32[512,256]{1,0:T(8,128)S(1)} %shard_map.63.refs_1_), custom_call_target="tpu_custom_call" | custom-call | flops 402653184 | bytes 2228224 | tf_op jit(solution)/shard_map/pallas_call | solution.py:45
  35.0 0.8 %collective-permute-start.6 = (bf16[2,128,512]{2,1,0:T(8,128)(2,1)S(1)}, bf16[2,128,512]{2,1,0:T(8,128)(2,1)S(1)}, u32[]{:S(2)}, u32[]{:S(2)}) collective-permute-start(bf16[2,128,512]{2,1,0:T(8,128)(2,1)S(1)} %shard_map.67), channel_id=1, source_target_pairs={{0,2},{1,3},{2,0},{3,1},{4,6},{5,7},{6,4},{7,5},{8,10},{9,11},{10,... | collective-permute-start | bytes 786440 | tf_op jit(solution)/shard_map/ppermute | solution.py:423
  36.2 0.7 %shard_map.66.own_ref = f32[2,128,2048]{2,1,0:T(8,128)S(1)} custom-call(bf16[2,128,512]{2,1,0:T(8,128)(2,1)S(1)} %shard_map.65.kept_ref, bf16[512,2048]{1,0:T(8,128)(2,1)S(1)} %copy-done), custom_call_target="tpu_custom_call" | custom-call | flops 536870912 | bytes 2359296 | tf_op jit(solution)/shard_map/pallas_call | solution.py:45
  37.0 7.9 %collective-permute-done.12.refs_5_ = bf16[64,2048]{1,0:T(8,128)(2,1)S(1)} collective-permute-done((bf16[64,2048]{1,0:T(8,128)(2,1)S(1)}, bf16[64,2048]{1,0:T(8,128)(2,1)S(1)}, u32[]{:S(2)}, u32[]{:S(2)}) %collective-permute-start.12) | collective-permute-done | bytes 262176 | tf_op jit(solution)/shard_map/ppermute | solution.py:423
  45.1 0.5 shard_map.70
  46.1 1.4 %collective-permute-done.14 = bf16[128,2048]{1,0:T(8,128)(2,1)S(1)} collective-permute-done((bf16[128,2048]{1,0:T(8,128)(2,1)S(1)}, bf16[128,2048]{1,0:T(8,128)(2,1)S(1)}, u32[]{:S(2)}, u32[]{:S(2)}) %collective-permute-start.14) | collective-permute-done | bytes 524320 | tf_op jit(solution)/shard_map/ppermute | solution.py:423
  47.5 0.9 %add_convert_fusion = bf16[128,2048]{1,0:T(8,128)(2,1)} fusion(f32[128,2048]{1,0:T(8,128)S(1)} %shard_map.69, bf16[128,2048]{1,0:T(8,128)(2,1)S(1)} %collective-permute-done.14), kind=kLoop, calls=%fused_computation | loop fusion | flops 786432 | bytes 2097152 | tf_op jit(solution)/shard_map/convert_element_type | solution.py:486
  (27 shorter events, 3.0 us)
Async XLA Ops:
  2.0 8.5 %collective-permute-start = (bf16[784,128]{1,0:T(8,128)(2,1)S(1)}, bf16[784,128]{1,0:T(8,128)(2,1)S(1)}, u32[]{:S(2)}, u32[]{:S(2)}) collective-permute-start(bf16[784,128]{1,0:T(8,128)(2,1)S(1)} %get-tuple-element.31), channel_id=1, source_target_pairs={{0,4},{4,0},{8,12},{12,8},{16,20},{20,16},{24,28},{28,24},{1,5},{5... | collective-permute-start | bytes 602120 | tf_op jit(solution)/shard_map/ppermute | solution.py:423
  7.4 6.8 %collective-permute-start.3 = (bf16[512,128]{1,0:T(8,128)(2,1)S(1)}, bf16[512,128]{1,0:T(8,128)(2,1)S(1)}, u32[]{:S(2)}, u32[]{:S(2)}) collective-permute-start(bf16[512,128]{1,0:T(8,128)(2,1)S(1)} %get-tuple-element.39), channel_id=1, source_target_pairs={{0,4},{4,0},{8,12},{12,8},{16,20},{20,16},{24,28},{28,24},{1,5},{5... | collective-permute-start | bytes 393224 | tf_op jit(solution)/shard_map/ppermute | solution.py:423
  7.5 16.9 %collective-permute-start.7 = (bf16[80,2048]{1,0:T(8,128)(2,1)S(1)}, bf16[80,2048]{1,0:T(8,128)(2,1)S(1)}, u32[]{:S(2)}, u32[]{:S(2)}) collective-permute-start(bf16[80,2048]{1,0:T(8,128)(2,1)S(1)} %get-tuple-element.49), channel_id=1, source_target_pairs={{0,2},{1,3},{2,0},{3,1},{4,6},{5,7},{6,4},{7,5},{8,10},{9,11},{10,... | collective-permute-start | bytes 983048 | tf_op jit(solution)/shard_map/ppermute | solution.py:423
  9.4 17.0 %collective-permute-start.8 = (bf16[80,2048]{1,0:T(8,128)(2,1)S(1)}, bf16[80,2048]{1,0:T(8,128)(2,1)S(1)}, u32[]{:S(2)}, u32[]{:S(2)}) collective-permute-start(bf16[80,2048]{1,0:T(8,128)(2,1)S(1)} %get-tuple-element.50), channel_id=1, source_target_pairs={{0,2},{1,3},{2,0},{3,1},{4,6},{5,7},{6,4},{7,5},{8,10},{9,11},{10,... | collective-permute-start | bytes 983048 | tf_op jit(solution)/shard_map/ppermute | solution.py:423
  10.6 8.9 %collective-permute-start.1 = (bf16[784,128]{1,0:T(8,128)(2,1)S(1)}, bf16[784,128]{1,0:T(8,128)(2,1)S(1)}, u32[]{:S(2)}, u32[]{:S(2)}) collective-permute-start(bf16[784,128]{1,0:T(8,128)(2,1)S(1)} %get-tuple-element.33), channel_id=1, source_target_pairs={{0,8},{4,12},{8,0},{12,4},{16,24},{20,28},{24,16},{28,20},{1,9},{5... | collective-permute-start | bytes 602120 | tf_op jit(solution)/shard_map/ppermute | solution.py:423
  12.7 16.6 %collective-permute-start.9 = (bf16[64,2048]{1,0:T(8,128)(2,1)S(1)}, bf16[64,2048]{1,0:T(8,128)(2,1)S(1)}, u32[]{:S(2)}, u32[]{:S(2)}) collective-permute-start(bf16[64,2048]{1,0:T(8,128)(2,1)S(1)} %get-tuple-element.51), channel_id=1, source_target_pairs={{0,2},{1,3},{2,0},{3,1},{4,6},{5,7},{6,4},{7,5},{8,10},{9,11},{10,... | collective-permute-start | bytes 786440 | tf_op jit(solution)/shard_map/ppermute | solution.py:423
  14.4 5.0 %collective-permute-start.4 = (bf16[512,128]{1,0:T(8,128)(2,1)S(1)}, bf16[512,128]{1,0:T(8,128)(2,1)S(1)}, u32[]{:S(2)}, u32[]{:S(2)}) collective-permute-start(bf16[512,128]{1,0:T(8,128)(2,1)S(1)} %get-tuple-element.41), channel_id=1, source_target_pairs={{0,8},{4,12},{8,0},{12,4},{16,24},{20,28},{24,16},{28,20},{1,9},{5... | collective-permute-start | bytes 393224 | tf_op jit(solution)/shard_map/ppermute | solution.py:423
  19.8 14.7 %collective-permute-start.5 = (bf16[512,128]{1,0:T(8,128)(2,1)S(1)}, bf16[512,128]{1,0:T(8,128)(2,1)S(1)}, u32[]{:S(2)}, u32[]{:S(2)}) collective-permute-start(bf16[512,128]{1,0:T(8,128)(2,1)S(1)} %get-tuple-element.48), channel_id=1, source_target_pairs={{0,16},{4,20},{8,24},{12,28},{16,0},{20,4},{24,8},{28,12},{1,17},{... | collective-permute-start | bytes 393224 | tf_op jit(solution)/shard_map/ppermute | solution.py:423
  22.6 8.3 %collective-permute-start.2 = (bf16[272,128]{1,0:T(8,128)(2,1)S(1)}, bf16[272,128]{1,0:T(8,128)(2,1)S(1)}, u32[]{:S(2)}, u32[]{:S(2)}) collective-permute-start(bf16[272,128]{1,0:T(8,128)(2,1)S(1)} %get-tuple-element.36), channel_id=1, source_target_pairs={{0,16},{4,20},{8,24},{12,28},{16,0},{20,4},{24,8},{28,12},{1,17},{... | collective-permute-start | bytes 208904 | tf_op jit(solution)/shard_map/ppermute | solution.py:423
  24.3 20.6 %collective-permute-start.10 = (bf16[80,2048]{1,0:T(8,128)(2,1)S(1)}, bf16[80,2048]{1,0:T(8,128)(2,1)S(1)}, u32[]{:S(2)}, u32[]{:S(2)}) collective-permute-start(bf16[80,2048]{1,0:T(8,128)(2,1)S(1)} %collective-permute-done.7.refs_0_), channel_id=1, source_target_pairs={{0,4},{4,0},{8,12},{12,8},{16,20},{20,16},{24,28},{28,24},{1,5},{5... | collective-permute-start | bytes 983048 | tf_op jit(solution)/shard_map/ppermute | solution.py:423
  26.4 18.5 %collective-permute-start.11 = (bf16[80,2048]{1,0:T(8,128)(2,1)S(1)}, bf16[80,2048]{1,0:T(8,128)(2,1)S(1)}, u32[]{:S(2)}, u32[]{:S(2)}) collective-permute-start(bf16[80,2048]{1,0:T(8,128)(2,1)S(1)} %collective-permute-done.8.refs_1_), channel_id=1, source_target_pairs={{0,4},{4,0},{8,12},{12,8},{16,20},{20,16},{24,28},{28,24},{1,5},{5... | collective-permute-start | bytes 983048 | tf_op jit(solution)/shard_map/ppermute | solution.py:423
  28.5 6.0 %copy-start.1 = (f32[512]{0:T(512)S(1)}, f32[512]{0:T(512)}, u32[]{:S(2)}) copy-start(f32[512]{0:T(512)} %param.8) | copy-start | bytes 6148
  29.3 7.7 %collective-permute-start.13 = (bf16[64,2048]{1,0:T(8,128)(2,1)S(1)}, bf16[64,2048]{1,0:T(8,128)(2,1)S(1)}, u32[]{:S(2)}, u32[]{:S(2)}) collective-permute-start(bf16[64,2048]{1,0:T(8,128)(2,1)S(1)} %get-tuple-element.52), channel_id=1, source_target_pairs={{0,2},{1,3},{2,0},{3,1},{4,6},{5,7},{6,4},{7,5},{8,10},{9,11},{10,... | collective-permute-start | bytes 786440 | tf_op jit(solution)/shard_map/ppermute | solution.py:423
  31.0 13.9 %collective-permute-start.12 = (bf16[64,2048]{1,0:T(8,128)(2,1)S(1)}, bf16[64,2048]{1,0:T(8,128)(2,1)S(1)}, u32[]{:S(2)}, u32[]{:S(2)}) collective-permute-start(bf16[64,2048]{1,0:T(8,128)(2,1)S(1)} %collective-permute-done.9.refs_2_), channel_id=1, source_target_pairs={{0,4},{4,0},{8,12},{12,8},{16,20},{20,16},{24,28},{28,24},{1,5},{5... | collective-permute-start | bytes 786440 | tf_op jit(solution)/shard_map/ppermute | solution.py:423
  34.5 1.7 %copy-start = (bf16[512,2048]{1,0:T(8,128)(2,1)S(1)}, bf16[512,2048]{1,0:T(8,128)(2,1)}, u32[]{:S(2)}) copy-start(bf16[512,2048]{1,0:T(8,128)(2,1)} %w_ref.1) | copy-start | bytes 6291460
  35.0 10.1 %collective-permute-start.6 = (bf16[2,128,512]{2,1,0:T(8,128)(2,1)S(1)}, bf16[2,128,512]{2,1,0:T(8,128)(2,1)S(1)}, u32[]{:S(2)}, u32[]{:S(2)}) collective-permute-start(bf16[2,128,512]{2,1,0:T(8,128)(2,1)S(1)} %shard_map.67), channel_id=1, source_target_pairs={{0,2},{1,3},{2,0},{3,1},{4,6},{5,7},{6,4},{7,5},{8,10},{9,11},{10,... | collective-permute-start | bytes 786440 | tf_op jit(solution)/shard_map/ppermute | solution.py:423
  45.5 2.0 %collective-permute-start.14 = (bf16[128,2048]{1,0:T(8,128)(2,1)S(1)}, bf16[128,2048]{1,0:T(8,128)(2,1)S(1)}, u32[]{:S(2)}, u32[]{:S(2)}) collective-permute-start(bf16[128,2048]{1,0:T(8,128)(2,1)S(1)} %shard_map.70), channel_id=1, source_target_pairs={{0,1},{1,0},{2,3},{3,2},{4,5},{5,4},{6,7},{7,6},{8,9},{9,8},{10,11... | collective-permute-start | bytes 1572872 | tf_op jit(solution)/shard_map/ppermute | solution.py:423

commit v2 on v1

--- a/solution.py
+++ b/solution.py
@@ -131,7 +131,7 @@
 def local_sums(q, k, v, weight, sizes):
     rows, width = q.shape
     heads = width // DH
-    chunks = 2 if rows % 32 == 0 else 1
+    chunks = 1
     return call(
         functools.partial(sums_kernel, chunks),
         [(a, pltpu.HBM) for a in (q, k, v, weight)],
@@ -332,7 +332,7 @@
     )[0]
 
 
-def normed_kernel(bit, blocks, other, q_ref, part_ref, base_ref, got_ref, gain_ref, out_ref):
+def normed_kernel(bit, blocks, other, q_ref, part_ref, base_ref, got_ref, gain_ref, *out_refs):
     weight = is_upper(bit).astype(F32)
     size = q_ref.shape[0] // blocks
     first = lax.bitwise_xor(lax.axis_index("head"), other)
@@ -343,7 +343,7 @@
             attended = part_ref[at, columns(h)] + mm(q_ref[at, columns(h)], pair)
             mean = jnp.mean(attended * attended, axis=-1, keepdims=True)
             normed = attended * lax.rsqrt(mean + 1e-6) * gain_ref[:, columns(h)]
-            out_ref[j, :, columns(h)] = normed.astype(BF16)
+            out_refs[j][:, columns(h)] = normed.astype(BF16)
 
 
 def normed_blocks(bit, other, q, part, base, got, gain, blocks):
@@ -351,9 +351,9 @@
     return call(
         functools.partial(normed_kernel, bit, blocks, other),
         vm(q, part, base, got, gain),
-        [((blocks // 2, rows // blocks, width), BF16)],
+        [((rows // blocks, width), BF16)] * (blocks // 2),
         flops=rows * width * DH,
-    )[0]
+    )
 
 
 def weights_kernel(shares, *refs):
@@ -377,43 +377,46 @@
     )[0]
 
 
-def project_own_kernel(kept_ref, w_ref, out_ref):
-    blocks, size, width = kept_ref.shape
-    kept = kept_ref[...].reshape(blocks * size, width)
-    span = out_ref.shape[2]
+def project_own_kernel(w_ref, *refs):
+    count = len(refs) // 2
+    span = w_ref.shape[1]
     tile = 512 if span % 512 == 0 else span
+    kept = jnp.concatenate([ref[...] for ref in refs[:count]], axis=0)
+    size = kept.shape[0] // count
     for start in range(0, span, tile):
         at = slice(start, start + tile)
-        out_ref[:, :, at] = mm(kept, w_ref[:, at]).reshape(blocks, size, tile)
+        total = mm(kept, w_ref[:, at])
+        for n, out_ref in enumerate(refs[count:]):
+            out_ref[:, at] = total[n * size : (n + 1) * size]
 
 
 def project_own(kept, weight):
-    blocks, size, width = kept.shape
+    size, width = kept[0].shape
     span = weight.shape[1]
     return call(
         project_own_kernel,
-        vm(kept, weight),
-        [((blocks, size, span), F32)],
-        flops=2 * blocks * size * width * span,
+        vm(weight, *kept),
+        [((size, span), F32)] * len(kept),
+        flops=2 * len(kept) * size * width * span,
         mib=8,
-    )[0]
-
-
-def project_kernel(index, own_ref, came_ref, w_ref, out_ref):
+    )
+
+
+def project_kernel(own_ref, came_ref, w_ref, out_ref):
     span = out_ref.shape[1]
     tile = 512 if span % 512 == 0 else span
     for start in range(0, span, tile):
         at = slice(start, start + tile)
-        out_ref[:, at] = (own_ref[index, :, at] + mm(came_ref[index], w_ref[:, at])).astype(out_ref.dtype)
-
-
-def project(index, own, came, weight, dtype):
-    _, size, span = own.shape
-    return call(
-        functools.partial(project_kernel, index),
+        out_ref[:, at] = (own_ref[:, at] + mm(came_ref[...], w_ref[:, at])).astype(out_ref.dtype)
+
+
+def project(own, came, weight, dtype):
+    size, span = own.shape
+    return call(
+        project_kernel,
         vm(own, came, weight),
         [((size, span), dtype)],
-        flops=2 * size * came.shape[2] * span,
+        flops=2 * size * came.shape[1] * span,
         mib=8,
     )[0]
 
@@ -467,16 +470,15 @@
 
     gain = norm_gain.reshape(1, width)
     sent = normed_blocks(bit, top, q, part, base, pairs_got, gain, head_count)
-    came = flip(sent, "head", top)
+    came = [flip(rows_sent, "head", top) for rows_sent in sent]
     kept = normed_blocks(bit, 0, q, part, base, pairs_got, gain, head_count)
     own = project_own(kept, out_weight)
     weight_came = join_weights(direct, neighbour, rest)
 
     count = top
-    if count == 1:
-        return project(0, own, came, weight_came, BF16)
     results = {
-        j: project(j, own, came, weight_came, BF16 if 2 * j >= count else F32) for j in reversed(range(count))
+        j: project(own[j], came[j], weight_came, BF16 if 2 * j >= count else F32)
+        for j in reversed(range(count))
     }
     while count > 1:
         count //= 2

time: 48.5 us -> 47.4 us (0.977)
  waiting for transfers between devices: 15.7 us -> 11.2 us
  starting transfers between devices: 19.2 us -> 22.5 us
    ppermute x15 -> x16, waiting for transfers between devices: 15.7 us -> 11.2 us  [flip(): return lax.ppermute(value, axis, [(i, i ^ bit) for i in range(count)])]
    ppermute x15 -> x16, starting transfers between devices: 19.2 us -> 22.5 us  [flip(): return lax.ppermute(value, axis, [(i, i ^ bit) for i in range(count)])]
  transfers between devices with their start and end apart: 15 -> 16, of which waited for: 6 -> 8; matrix products, arithmetic and copies ran while one was open for 0% -> 0% of each run, Pallas kernels for 21% -> 21%
where the time goes in v2:
time: 47.4 us; the launch traced here: 47.2 us
  starting transfers between devices  22.5 us (47%)
  Pallas kernels  12.2 us (26%)
  waiting for transfers between devices  11.2 us (24%)
  other arithmetic  0.9 us (2%)
    ppermute x16, starting transfers between devices, flip(): return lax.ppermute(value, axis, [(i, i ^ bit) for i in range(count)])  22.5 us
    pallas_call x16, Pallas kernels, call(): pl.pallas_call(kernel, in_specs=[pl.BlockSpec(memory_space=space) for a,...  12.2 us
    ppermute x16, waiting for transfers between devices, flip(): return lax.ppermute(value, axis, [(i, i ^ bit) for i in range(count)])  11.2 us
  transfers between devices with their start and end apart: 16, of which 8 were waited for; matrix products, arithmetic and copies ran while one was open for 0% of the time, Pallas kernels for 21%

profile of v2, /device:TPU:0, one launch (start us, length us, event | category | flops | bytes accessed | tf_op | source)
XLA Modules:
  0.0 47.2 jit_solution(10259630124051525315)
XLA Ops:
  0.0 1.8 %shard_map.55 = (bf16[512,512]{1,0:T(8,128)(2,1)S(1)}, bf16[512,512]{1,0:T(8,128)(2,1)S(1)}, bf16[512,512]{1,0:T(8,128)(2,1)S(1)}, f32[784,128]{1,0:T(8,128)S(1)...) custom-call(bf16[512,512]{1,0:T(8,128)(2,1)} %q_hbm.1, ...), custom_call_target="tpu_custom_call" | custom-call | flops 134217728 | bytes 3670016 | tf_op jit(solution)/shard_map/pallas_call | solution.py:45
  1.8 3.1 %collective-permute-start = (bf16[784,128]{1,0:T(8,128)(2,1)S(1)}, bf16[784,128]{1,0:T(8,128)(2,1)S(1)}, u32[]{:S(2)}, u32[]{:S(2)}) collective-permute-start(bf16[784,128]{1,0:T(8,128)(2,1)S(1)} %get-tuple-element.37), channel_id=1, source_target_pairs={{0,4},{4,0},{8,12},{12,8},{16,20},{20,16},{24,28},{28,24},{1,5},{5... | collective-permute-start | bytes 602120 | tf_op jit(solution)/shard_map/ppermute | solution.py:426
  4.9 1.5 %collective-permute-start.7 = (bf16[80,2048]{1,0:T(8,128)(2,1)S(1)}, bf16[80,2048]{1,0:T(8,128)(2,1)S(1)}, u32[]{:S(2)}, u32[]{:S(2)}) collective-permute-start(bf16[80,2048]{1,0:T(8,128)(2,1)S(1)} %get-tuple-element.59), channel_id=1, source_target_pairs={{0,2},{1,3},{2,0},{3,1},{4,6},{5,7},{6,4},{7,5},{8,10},{9,11},{10,... | collective-permute-start | bytes 983048 | tf_op jit(solution)/shard_map/ppermute | solution.py:426
  6.9 2.3 %shard_map.58 = (f32[4,128,128]{2,1,0:T(8,128)S(1)}, bf16[512,128]{1,0:T(8,128)(2,1)S(1)}, bf16[4,512,512]{2,1,0:T(8,128)(2,1)S(1)}, bf16[64,2048]{1,0:T(8,128)(2,1)S(1)}) custom-call(bf16[512,512]{1,0:T(8,128)(2,1)S(1)} %get-tuple-element.35.q_ref, bf16[512,512]{1,0:T(8,128)(2,1)S(1)} %get-tuple-element.44.k_ref, ...), custom_call_target="tpu_custom_call" | custom-call | flops 268435456 | bytes 3670016 | tf_op jit(solution)/shard_map/pallas_call | solution.py:45
  9.9 1.9 %collective-permute-start.1 = (bf16[784,128]{1,0:T(8,128)(2,1)S(1)}, bf16[784,128]{1,0:T(8,128)(2,1)S(1)}, u32[]{:S(2)}, u32[]{:S(2)}) collective-permute-start(bf16[784,128]{1,0:T(8,128)(2,1)S(1)} %get-tuple-element.39), channel_id=1, source_target_pairs={{0,8},{4,12},{8,0},{12,4},{16,24},{20,28},{24,16},{28,20},{1,9},{5... | collective-permute-start | bytes 602120 | tf_op jit(solution)/shard_map/ppermute | solution.py:426
  11.8 1.5 %collective-permute-start.9 = (bf16[64,2048]{1,0:T(8,128)(2,1)S(1)}, bf16[64,2048]{1,0:T(8,128)(2,1)S(1)}, u32[]{:S(2)}, u32[]{:S(2)}) collective-permute-start(bf16[64,2048]{1,0:T(8,128)(2,1)S(1)} %get-tuple-element.61), channel_id=1, source_target_pairs={{0,2},{1,3},{2,0},{3,1},{4,6},{5,7},{6,4},{7,5},{8,10},{9,11},{10,... | collective-permute-start | bytes 786440 | tf_op jit(solution)/shard_map/ppermute | solution.py:426
  13.3 1.0 %collective-permute-done.3.got_ref = bf16[512,128]{1,0:T(8,128)(2,1)S(1)} collective-permute-done((bf16[512,128]{1,0:T(8,128)(2,1)S(1)}, bf16[512,128]{1,0:T(8,128)(2,1)S(1)}, u32[]{:S(2)}, u32[]{:S(2)}) %collective-permute-start.3) | collective-permute-done | bytes 131104 | tf_op jit(solution)/shard_map/ppermute | solution.py:426
  14.5 1.6 %collective-permute-start.4 = (bf16[512,128]{1,0:T(8,128)(2,1)S(1)}, bf16[512,128]{1,0:T(8,128)(2,1)S(1)}, u32[]{:S(2)}, u32[]{:S(2)}) collective-permute-start(bf16[512,128]{1,0:T(8,128)(2,1)S(1)} %get-tuple-element.47), channel_id=1, source_target_pairs={{0,8},{4,12},{8,0},{12,4},{16,24},{20,28},{24,16},{28,20},{1,9},{5... | collective-permute-start | bytes 393224 | tf_op jit(solution)/shard_map/ppermute | solution.py:426
  16.1 0.9 %collective-permute-done.1.got_ref.sums_got_ref = bf16[784,128]{1,0:T(8,128)(2,1)S(1)} collective-permute-done((bf16[784,128]{1,0:T(8,128)(2,1)S(1)}, bf16[784,128]{1,0:T(8,128)(2,1)S(1)}, u32[]{:S(2)}, u32[]{:S(2)}) %collective-permute-start.1) | collective-permute-done | bytes 200736 | tf_op jit(solution)/shard_map/ppermute | solution.py:426
  17.1 2.5 %collective-permute-start.2 = (bf16[272,128]{1,0:T(8,128)(2,1)S(1)}, bf16[272,128]{1,0:T(8,128)(2,1)S(1)}, u32[]{:S(2)}, u32[]{:S(2)}) collective-permute-start(bf16[272,128]{1,0:T(8,128)(2,1)S(1)} %get-tuple-element.42), channel_id=1, source_target_pairs={{0,16},{4,20},{8,24},{12,28},{16,0},{20,4},{24,8},{28,12},{1,17},{... | collective-permute-start | bytes 208904 | tf_op jit(solution)/shard_map/ppermute | solution.py:426
  19.6 2.4 %collective-permute-start.10 = (bf16[80,2048]{1,0:T(8,128)(2,1)S(1)}, bf16[80,2048]{1,0:T(8,128)(2,1)S(1)}, u32[]{:S(2)}, u32[]{:S(2)}) collective-permute-start(bf16[80,2048]{1,0:T(8,128)(2,1)S(1)} %collective-permute-done.7.refs_0_), channel_id=1, source_target_pairs={{0,4},{4,0},{8,12},{12,8},{16,20},{20,16},{24,28},{28,24},{1,5},{5... | collective-permute-start | bytes 983048 | tf_op jit(solution)/shard_map/ppermute | solution.py:426
  22.9 3.1 %collective-permute-start.5 = (bf16[512,128]{1,0:T(8,128)(2,1)S(1)}, bf16[512,128]{1,0:T(8,128)(2,1)S(1)}, u32[]{:S(2)}, u32[]{:S(2)}) collective-permute-start(bf16[512,128]{1,0:T(8,128)(2,1)S(1)} %get-tuple-element.54), channel_id=1, source_target_pairs={{0,16},{4,20},{8,24},{12,28},{16,0},{20,4},{24,8},{28,12},{1,17},{... | collective-permute-start | bytes 393224 | tf_op jit(solution)/shard_map/ppermute | solution.py:426
  26.0 0.7 %collective-permute-done.9.refs_2_ = bf16[64,2048]{1,0:T(8,128)(2,1)S(1)} collective-permute-done((bf16[64,2048]{1,0:T(8,128)(2,1)S(1)}, bf16[64,2048]{1,0:T(8,128)(2,1)S(1)}, u32[]{:S(2)}, u32[]{:S(2)}) %collective-permute-start.9) | collective-permute-done | bytes 262176 | tf_op jit(solution)/shard_map/ppermute | solution.py:426
  26.7 1.5 %collective-permute-start.13 = (bf16[64,2048]{1,0:T(8,128)(2,1)S(1)}, bf16[64,2048]{1,0:T(8,128)(2,1)S(1)}, u32[]{:S(2)}, u32[]{:S(2)}) collective-permute-start(bf16[64,2048]{1,0:T(8,128)(2,1)S(1)} %get-tuple-element.62), channel_id=1, source_target_pairs={{0,2},{1,3},{2,0},{3,1},{4,6},{5,7},{6,4},{7,5},{8,10},{9,11},{10,... | collective-permute-start | bytes 786440 | tf_op jit(solution)/shard_map/ppermute | solution.py:426
  28.2 0.8 %collective-permute-start.12 = (bf16[64,2048]{1,0:T(8,128)(2,1)S(1)}, bf16[64,2048]{1,0:T(8,128)(2,1)S(1)}, u32[]{:S(2)}, u32[]{:S(2)}) collective-permute-start(bf16[64,2048]{1,0:T(8,128)(2,1)S(1)} %collective-permute-done.9.refs_2_), channel_id=1, source_target_pairs={{0,4},{4,0},{8,12},{12,8},{16,20},{20,16},{24,28},{28,24},{1,5},{5... | collective-permute-start | bytes 786440 | tf_op jit(solution)/shard_map/ppermute | solution.py:426
  29.0 1.4 %shard_map.63.refs_1_ = f32[512,256]{1,0:T(8,128)S(1)} custom-call(bf16[512,512]{1,0:T(8,128)(2,1)S(1)} %get-tuple-element.35.q_ref, bf16[512,512]{1,0:T(8,128)(2,1)S(1)} %get-tuple-element.44.k_ref, bf16[512,512]{1,0:T(8,128)(2,1)S(1)} %get-tuple-element.36.v_ref, bf16[4,512,512]{2,1,0:T(8,128)(2,1)S(1)} %get-tuple-element.52.paired_ref), custom_call_target="tpu_custom_call" | custom-call | flops 268435456 | bytes 3670016 | tf_op jit(solution)/shard_map/pallas_call | solution.py:45
  30.4 1.4 %shard_map.62.refs_0_ = f32[512,256]{1,0:T(8,128)S(1)} custom-call(bf16[512,512]{1,0:T(8,128)(2,1)S(1)} %get-tuple-element.35.q_ref, bf16[512,512]{1,0:T(8,128)(2,1)S(1)} %get-tuple-element.44.k_ref, bf16[512,512]{1,0:T(8,128)(2,1)S(1)} %get-tuple-element.36.v_ref, bf16[4,512,512]{2,1,0:T(8,128)(2,1)S(1)} %get-tuple-element.52.paired_ref), custom_call_target="tpu_custom_call" | custom-call | flops 268435456 | bytes 3670016 | tf_op jit(solution)/shard_map/pallas_call | solution.py:45
  32.1 1.8 %shard_map.64.part_ref = f32[512,512]{1,0:T(8,128)S(1)} custom-call(bf16[512,512]{1,0:T(8,128)(2,1)S(1)} %get-tuple-element.35.q_ref, bf16[512,512]{1,0:T(8,128)(2,1)S(1)} %get-tuple-element.36.v_ref, bf16[4,128,128]{2,1,0:T(8,128)(2,1)S(1)} %get-tuple-element.51.gram_ref, f32[512,256]{1,0:T(8,128)S(1)} %shard_map.62.refs_0_, f32[512,256]{1,0:T(8,128)S(1)} %shard_map.63.refs_1_), custom_call_target="tpu_custom_call" | custom-call | flops 402653184 | bytes 2228224 | tf_op jit(solution)/shard_map/pallas_call | solution.py:45
  34.3 0.6 %collective-permute-start.14 = (bf16[128,512]{1,0:T(8,128)(2,1)S(1)}, bf16[128,512]{1,0:T(8,128)(2,1)S(1)}, u32[]{:S(2)}, u32[]{:S(2)}) collective-permute-start(bf16[128,512]{1,0:T(8,128)(2,1)S(1)} %get-tuple-element.64), channel_id=1, source_target_pairs={{0,2},{1,3},{2,0},{3,1},{4,6},{5,7},{6,4},{7,5},{8,10},{9,11},{10,... | collective-permute-start | bytes 393224 | tf_op jit(solution)/shard_map/ppermute | solution.py:426
  35.5 0.7 %shard_map.66 = (f32[128,2048]{1,0:T(8,128)S(1)}, f32[128,2048]{1,0:T(8,128)S(1)}) custom-call(bf16[512,2048]{1,0:T(8,128)(2,1)S(1)} %copy-done, bf16[128,512]{1,0:T(8,128)(2,1)S(1)} %get-tuple-element.55.refs_0_, bf16[128,512]{1,0:T(8,128)(2,1)S(1)} %get-tuple-element.56.refs_1_), custom_call_target="tpu_custom_call" | custom-call | flops 536870912 | bytes 2359296 | tf_op jit(solution)/shard_map/pallas_call | solution.py:45
  36.2 2.7 %collective-permute-done.12.refs_5_ = bf16[64,2048]{1,0:T(8,128)(2,1)S(1)} collective-permute-done((bf16[64,2048]{1,0:T(8,128)(2,1)S(1)}, bf16[64,2048]{1,0:T(8,128)(2,1)S(1)}, u32[]{:S(2)}, u32[]{:S(2)}) %collective-permute-start.12) | collective-permute-done | bytes 262176 | tf_op jit(solution)/shard_map/ppermute | solution.py:426
  39.9 1.3 %collective-permute-start.6 = (bf16[128,512]{1,0:T(8,128)(2,1)S(1)}, bf16[128,512]{1,0:T(8,128)(2,1)S(1)}, u32[]{:S(2)}, u32[]{:S(2)}) collective-permute-start(bf16[128,512]{1,0:T(8,128)(2,1)S(1)} %get-tuple-element.58), channel_id=1, source_target_pairs={{0,2},{1,3},{2,0},{3,1},{4,6},{5,7},{6,4},{7,5},{8,10},{9,11},{10,... | collective-permute-start | bytes 393224 | tf_op jit(solution)/shard_map/ppermute | solution.py:426
  41.2 4.6 %collective-permute-done.6.came_ref = bf16[128,512]{1,0:T(8,128)(2,1)S(1)} collective-permute-done((bf16[128,512]{1,0:T(8,128)(2,1)S(1)}, bf16[128,512]{1,0:T(8,128)(2,1)S(1)}, u32[]{:S(2)}, u32[]{:S(2)}) %collective-permute-start.6) | collective-permute-done | bytes 131104 | tf_op jit(solution)/shard_map/ppermute | solution.py:426
  46.3 0.9 %add_convert_fusion = bf16[128,2048]{1,0:T(8,128)(2,1)} fusion(f32[128,2048]{1,0:T(8,128)S(1)} %shard_map.69, bf16[128,2048]{1,0:T(8,128)(2,1)S(1)} %collective-permute-done.15), kind=kLoop, calls=%fused_computation | loop fusion | flops 786432 | bytes 2097152 | tf_op jit(solution)/shard_map/convert_element_type | solution.py:488
  (29 shorter events, 5.1 us)
Async XLA Ops:
  1.8 8.0 %collective-permute-start = (bf16[784,128]{1,0:T(8,128)(2,1)S(1)}, bf16[784,128]{1,0:T(8,128)(2,1)S(1)}, u32[]{:S(2)}, u32[]{:S(2)}) collective-permute-start(bf16[784,128]{1,0:T(8,128)(2,1)S(1)} %get-tuple-element.37), channel_id=1, source_target_pairs={{0,4},{4,0},{8,12},{12,8},{16,20},{20,16},{24,28},{28,24},{1,5},{5... | collective-permute-start | bytes 602120 | tf_op jit(solution)/shard_map/ppermute | solution.py:426
  4.9 14.7 %collective-permute-start.7 = (bf16[80,2048]{1,0:T(8,128)(2,1)S(1)}, bf16[80,2048]{1,0:T(8,128)(2,1)S(1)}, u32[]{:S(2)}, u32[]{:S(2)}) collective-permute-start(bf16[80,2048]{1,0:T(8,128)(2,1)S(1)} %get-tuple-element.59), channel_id=1, source_target_pairs={{0,2},{1,3},{2,0},{3,1},{4,6},{5,7},{6,4},{7,5},{8,10},{9,11},{10,... | collective-permute-start | bytes 983048 | tf_op jit(solution)/shard_map/ppermute | solution.py:426
  6.4 16.1 %collective-permute-start.8 = (bf16[80,2048]{1,0:T(8,128)(2,1)S(1)}, bf16[80,2048]{1,0:T(8,128)(2,1)S(1)}, u32[]{:S(2)}, u32[]{:S(2)}) collective-permute-start(bf16[80,2048]{1,0:T(8,128)(2,1)S(1)} %get-tuple-element.60), channel_id=1, source_target_pairs={{0,2},{1,3},{2,0},{3,1},{4,6},{5,7},{6,4},{7,5},{8,10},{9,11},{10,... | collective-permute-start | bytes 983048 | tf_op jit(solution)/shard_map/ppermute | solution.py:426
  9.2 5.0 %collective-permute-start.3 = (bf16[512,128]{1,0:T(8,128)(2,1)S(1)}, bf16[512,128]{1,0:T(8,128)(2,1)S(1)}, u32[]{:S(2)}, u32[]{:S(2)}) collective-permute-start(bf16[512,128]{1,0:T(8,128)(2,1)S(1)} %get-tuple-element.45), channel_id=1, source_target_pairs={{0,4},{4,0},{8,12},{12,8},{16,20},{20,16},{24,28},{28,24},{1,5},{5... | collective-permute-start | bytes 393224 | tf_op jit(solution)/shard_map/ppermute | solution.py:426
  9.9 7.1 %collective-permute-start.1 = (bf16[784,128]{1,0:T(8,128)(2,1)S(1)}, bf16[784,128]{1,0:T(8,128)(2,1)S(1)}, u32[]{:S(2)}, u32[]{:S(2)}) collective-permute-start(bf16[784,128]{1,0:T(8,128)(2,1)S(1)} %get-tuple-element.39), channel_id=1, source_target_pairs={{0,8},{4,12},{8,0},{12,4},{16,24},{20,28},{24,16},{28,20},{1,9},{5... | collective-permute-start | bytes 602120 | tf_op jit(solution)/shard_map/ppermute | solution.py:426
  11.8 14.9 %collective-permute-start.9 = (bf16[64,2048]{1,0:T(8,128)(2,1)S(1)}, bf16[64,2048]{1,0:T(8,128)(2,1)S(1)}, u32[]{:S(2)}, u32[]{:S(2)}) collective-permute-start(bf16[64,2048]{1,0:T(8,128)(2,1)S(1)} %get-tuple-element.61), channel_id=1, source_target_pairs={{0,2},{1,3},{2,0},{3,1},{4,6},{5,7},{6,4},{7,5},{8,10},{9,11},{10,... | collective-permute-start | bytes 786440 | tf_op jit(solution)/shard_map/ppermute | solution.py:426
  14.5 8.1 %collective-permute-start.4 = (bf16[512,128]{1,0:T(8,128)(2,1)S(1)}, bf16[512,128]{1,0:T(8,128)(2,1)S(1)}, u32[]{:S(2)}, u32[]{:S(2)}) collective-permute-start(bf16[512,128]{1,0:T(8,128)(2,1)S(1)} %get-tuple-element.47), channel_id=1, source_target_pairs={{0,8},{4,12},{8,0},{12,4},{16,24},{20,28},{24,16},{28,20},{1,9},{5... | collective-permute-start | bytes 393224 | tf_op jit(solution)/shard_map/ppermute | solution.py:426
  17.1 11.1 %collective-permute-start.2 = (bf16[272,128]{1,0:T(8,128)(2,1)S(1)}, bf16[272,128]{1,0:T(8,128)(2,1)S(1)}, u32[]{:S(2)}, u32[]{:S(2)}) collective-permute-start(bf16[272,128]{1,0:T(8,128)(2,1)S(1)} %get-tuple-element.42), channel_id=1, source_target_pairs={{0,16},{4,20},{8,24},{12,28},{16,0},{20,4},{24,8},{28,12},{1,17},{... | collective-permute-start | bytes 208904 | tf_op jit(solution)/shard_map/ppermute | solution.py:426
  19.6 19.3 %collective-permute-start.10 = (bf16[80,2048]{1,0:T(8,128)(2,1)S(1)}, bf16[80,2048]{1,0:T(8,128)(2,1)S(1)}, u32[]{:S(2)}, u32[]{:S(2)}) collective-permute-start(bf16[80,2048]{1,0:T(8,128)(2,1)S(1)} %collective-permute-done.7.refs_0_), channel_id=1, source_target_pairs={{0,4},{4,0},{8,12},{12,8},{16,20},{20,16},{24,28},{28,24},{1,5},{5... | collective-permute-start | bytes 983048 | tf_op jit(solution)/shard_map/ppermute | solution.py:426
  22.5 16.4 %collective-permute-start.11 = (bf16[80,2048]{1,0:T(8,128)(2,1)S(1)}, bf16[80,2048]{1,0:T(8,128)(2,1)S(1)}, u32[]{:S(2)}, u32[]{:S(2)}) collective-permute-start(bf16[80,2048]{1,0:T(8,128)(2,1)S(1)} %collective-permute-done.8.refs_1_), channel_id=1, source_target_pairs={{0,4},{4,0},{8,12},{12,8},{16,20},{20,16},{24,28},{28,24},{1,5},{5... | collective-permute-start | bytes 983048 | tf_op jit(solution)/shard_map/ppermute | solution.py:426
  22.9 11.0 %collective-permute-start.5 = (bf16[512,128]{1,0:T(8,128)(2,1)S(1)}, bf16[512,128]{1,0:T(8,128)(2,1)S(1)}, u32[]{:S(2)}, u32[]{:S(2)}) collective-permute-start(bf16[512,128]{1,0:T(8,128)(2,1)S(1)} %get-tuple-element.54), channel_id=1, source_target_pairs={{0,16},{4,20},{8,24},{12,28},{16,0},{20,4},{24,8},{28,12},{1,17},{... | collective-permute-start | bytes 393224 | tf_op jit(solution)/shard_map/ppermute | solution.py:426
  26.7 9.5 %collective-permute-start.13 = (bf16[64,2048]{1,0:T(8,128)(2,1)S(1)}, bf16[64,2048]{1,0:T(8,128)(2,1)S(1)}, u32[]{:S(2)}, u32[]{:S(2)}) collective-permute-start(bf16[64,2048]{1,0:T(8,128)(2,1)S(1)} %get-tuple-element.62), channel_id=1, source_target_pairs={{0,2},{1,3},{2,0},{3,1},{4,6},{5,7},{6,4},{7,5},{8,10},{9,11},{10,... | collective-permute-start | bytes 786440 | tf_op jit(solution)/shard_map/ppermute | solution.py:426
  28.2 10.7 %collective-permute-start.12 = (bf16[64,2048]{1,0:T(8,128)(2,1)S(1)}, bf16[64,2048]{1,0:T(8,128)(2,1)S(1)}, u32[]{:S(2)}, u32[]{:S(2)}) collective-permute-start(bf16[64,2048]{1,0:T(8,128)(2,1)S(1)} %collective-permute-done.9.refs_2_), channel_id=1, source_target_pairs={{0,4},{4,0},{8,12},{12,8},{16,20},{20,16},{24,28},{28,24},{1,5},{5... | collective-permute-start | bytes 786440 | tf_op jit(solution)/shard_map/ppermute | solution.py:426
  31.9 2.1 %copy-start.1 = (f32[512]{0:T(512)S(1)}, f32[512]{0:T(512)}, u32[]{:S(2)}) copy-start(f32[512]{0:T(512)} %param.8) | copy-start | bytes 6148
  33.9 1.6 %copy-start = (bf16[512,2048]{1,0:T(8,128)(2,1)S(1)}, bf16[512,2048]{1,0:T(8,128)(2,1)}, u32[]{:S(2)}) copy-start(bf16[512,2048]{1,0:T(8,128)(2,1)} %w_ref.1) | copy-start | bytes 6291460
  34.3 5.0 %collective-permute-start.14 = (bf16[128,512]{1,0:T(8,128)(2,1)S(1)}, bf16[128,512]{1,0:T(8,128)(2,1)S(1)}, u32[]{:S(2)}, u32[]{:S(2)}) collective-permute-start(bf16[128,512]{1,0:T(8,128)(2,1)S(1)} %get-tuple-element.64), channel_id=1, source_target_pairs={{0,2},{1,3},{2,0},{3,1},{4,6},{5,7},{6,4},{7,5},{8,10},{9,11},{10,... | collective-permute-start | bytes 393224 | tf_op jit(solution)/shard_map/ppermute | solution.py:426
  39.8 6.4 %collective-permute-start.15 = (bf16[128,2048]{1,0:T(8,128)(2,1)S(1)}, bf16[128,2048]{1,0:T(8,128)(2,1)S(1)}, u32[]{:S(2)}, u32[]{:S(2)}) collective-permute-start(bf16[128,2048]{1,0:T(8,128)(2,1)S(1)} %shard_map.70), channel_id=1, source_target_pairs={{0,1},{1,0},{2,3},{3,2},{4,5},{5,4},{6,7},{7,6},{8,9},{9,8},{10,11... | collective-permute-start | bytes 1572872 | tf_op jit(solution)/shard_map/ppermute | solution.py:426
  39.9 5.9 %collective-permute-start.6 = (bf16[128,512]{1,0:T(8,128)(2,1)S(1)}, bf16[128,512]{1,0:T(8,128)(2,1)S(1)}, u32[]{:S(2)}, u32[]{:S(2)}) collective-permute-start(bf16[128,512]{1,0:T(8,128)(2,1)S(1)} %get-tuple-element.58), channel_id=1, source_target_pairs={{0,2},{1,3},{2,0},{3,1},{4,6},{5,7},{6,4},{7,5},{8,10},{9,11},{10,... | collective-permute-start | bytes 393224 | tf_op jit(solution)/shard_map/ppermute | solution.py:426

commit v3 on v2

--- a/solution.py
+++ b/solution.py
@@ -10,7 +10,7 @@
 
 DH = 128
 DIAG = 16
-SHARES = (5, 5, 4)
+SHARES = ((6, 1), (6, 1), (2, 2))
 F32 = jnp.float32
 BF16 = jnp.bfloat16
 
@@ -87,7 +87,27 @@
     return (heads + 1) // 2 * DH + DIAG
 
 
-def sums_kernel(chunks, q_hbm, k_hbm, v_hbm, w_hbm, q_ref, k_ref, v_ref, own_ref, send_ref, *refs):
+def share_places(sizes, bits):
+    places, at = [], 0
+    for bit in sorted(set(bits)):
+        region = sum(size for size, b in zip(sizes, bits) if b == bit)
+        skip = 0
+        for n, size in enumerate(sizes):
+            if bits[n] == bit:
+                places.append((n, (bit, at + skip, at + region + skip)))
+                skip += size
+        at += 2 * region
+    return [place for n, place in sorted(places)]
+
+
+def share_row(bit, low, high, other=False):
+    upper = is_upper(bit)
+    if other:
+        upper = jnp.logical_not(upper)
+    return pl.multiple_of(jnp.where(upper, high, low), 16)
+
+
+def sums_kernel(chunks, places, q_hbm, k_hbm, v_hbm, w_hbm, q_ref, k_ref, v_ref, own_ref, send_ref, *refs):
     *w_refs, sem, w_sem = refs
     rows, width = q_ref.shape
     heads = width // DH
@@ -97,11 +117,9 @@
         at = pl.ds(c * size, size)
         for n, (src, dst) in enumerate(((k_hbm, k_ref), (q_hbm, q_ref), (v_hbm, v_ref))):
             copies.append(pltpu.make_async_copy(src.at[at], dst.at[at], sem.at[c, n]))
-    sizes = [ref.shape[0] for ref in w_refs]
-    first = lax.bitwise_and(lax.axis_index("seq"), 1) * sum(sizes)
-    for n, w_ref in enumerate(w_refs):
-        at = pl.multiple_of(first + sum(sizes[:n]), 16)
-        copies.append(pltpu.make_async_copy(w_hbm.at[pl.ds(at, sizes[n])], w_ref, w_sem.at[n]))
+    for n, (w_ref, (bit, low, high)) in enumerate(zip(w_refs, places)):
+        at = share_row(bit, low, high)
+        copies.append(pltpu.make_async_copy(w_hbm.at[pl.ds(at, w_ref.shape[0])], w_ref, w_sem.at[n]))
     for copy in copies:
         copy.start()
     grams = [None] * heads
@@ -128,12 +146,12 @@
         copy.wait()
 
 
-def local_sums(q, k, v, weight, sizes):
+def local_sums(q, k, v, weight, sizes, places):
     rows, width = q.shape
     heads = width // DH
     chunks = 1
     return call(
-        functools.partial(sums_kernel, chunks),
+        functools.partial(sums_kernel, chunks, places),
         [(a, pltpu.HBM) for a in (q, k, v, weight)],
         [((rows, width), BF16)] * 3
         + [((packed_rows(heads) + heads * DH, DH), dtype) for dtype in (F32, BF16)]
@@ -356,21 +374,19 @@
     )
 
 
-def weights_kernel(shares, *refs):
+def weights_kernel(places, *refs):
     *parts, rest_ref, out_ref = refs
-    sizes = [ref.shape[0] for ref in parts[:shares]]
-    odd = lax.bitwise_and(lax.axis_index("seq"), 1)
-    for n, size in enumerate(sizes):
-        for first, ref in ((odd, parts[n]), (1 - odd, parts[shares + n])):
-            at = pl.multiple_of(first * sum(sizes) + sum(sizes[:n]), 16)
-            out_ref[pl.ds(at, size), :] = ref[...]
-    out_ref[pl.ds(2 * sum(sizes), rest_ref.shape[0]), :] = rest_ref[...]
-
-
-def join_weights(direct, neighbour, rest):
+    for n, place in enumerate(places):
+        for ref, other in ((parts[n], False), (parts[len(places) + n], True)):
+            out_ref[pl.ds(share_row(*place, other), ref.shape[0]), :] = ref[...]
+    left = rest_ref.shape[0]
+    out_ref[pl.ds(out_ref.shape[0] - left, left), :] = rest_ref[...]
+
+
+def join_weights(direct, neighbour, rest, places):
     rows = sum(part.shape[0] for part in (*direct, *neighbour, rest))
     return call(
-        functools.partial(weights_kernel, len(direct)),
+        functools.partial(weights_kernel, places),
         vm(*direct, *neighbour, rest),
         [((rows, rest.shape[1]), BF16)],
         mib=8,
@@ -433,16 +449,18 @@
 
     top = head_count // 2
     features = out_weight.shape[0]
-    sizes = [features * n // 32 // 16 * 16 for n in SHARES]
+    bits = [bit for n, bit in SHARES if bit < seq_count]
+    sizes = [features * n // 32 // 16 * 16 for n, bit in SHARES if bit < seq_count]
+    places = share_places(sizes, bits)
 
     q, k, v, sums, sums_send, *weight_shares = local_sums(
-        queries, key_vectors, value_vectors, out_weight, sizes
+        queries, key_vectors, value_vectors, out_weight, sizes, places
     )
     pairs, pairs_send, paired, weight_rest = local_pairs(
         q, k, v, out_weight, features - 2 * sum(sizes), block
     )
     direct = [flip(w, "head", top) for w in weight_shares]
-    neighbour = [flip(w, "seq", 1) for w in direct]
+    neighbour = [flip(w, "seq", bits[n]) for n, w in enumerate(direct)]
     rest = flip(weight_rest, "head", top)
     heads = width // DH
     parts = [
@@ -473,7 +491,7 @@
     came = [flip(rows_sent, "head", top) for rows_sent in sent]
     kept = normed_blocks(bit, 0, q, part, base, pairs_got, gain, head_count)
     own = project_own(kept, out_weight)
-    weight_came = join_weights(direct, neighbour, rest)
+    weight_came = join_weights(direct, neighbour, rest, places)
 
     count = top
     results = {

time: 47.4 us -> 53.1 us (1.12)
  waiting for transfers between devices: 11.2 us -> 14.6 us
  starting transfers between devices: 22.5 us -> 25 us
    ppermute x16, waiting for transfers between devices: 11.2 us -> 14.6 us  [flip(): return lax.ppermute(value, axis, [(i, i ^ bit) for i in range(count)])]
    ppermute x16, starting transfers between devices: 22.5 us -> 25 us  [flip(): return lax.ppermute(value, axis, [(i, i ^ bit) for i in range(count)])]
  transfers between devices with their start and end apart: 16 -> 16, of which waited for: 8 -> 6; matrix products, arithmetic and copies ran while one was open for 0% -> 0% of each run, Pallas kernels for 21% -> 19%
where the time goes in v3:
time: 53.1 us; the launch traced here: 53 us
  starting transfers between devices  25 us (47%)
  waiting for transfers between devices  14.6 us (27%)
  Pallas kernels  12.2 us (23%)
  other arithmetic  0.9 us (2%)
    ppermute x16, starting transfers between devices, flip(): return lax.ppermute(value, axis, [(i, i ^ bit) for i in range(count)])  25 us
    ppermute x16, waiting for transfers between devices, flip(): return lax.ppermute(value, axis, [(i, i ^ bit) for i in range(count)])  14.6 us
    pallas_call x16, Pallas kernels, call(): pl.pallas_call(kernel, in_specs=[pl.BlockSpec(memory_space=space) for a,...  12.2 us
  transfers between devices with their start and end apart: 16, of which 6 were waited for; matrix products, arithmetic and copies ran while one was open for 0% of the time, Pallas kernels for 19%

profile of v3, /device:TPU:0, one launch (start us, length us, event | category | flops | bytes accessed | tf_op | source)
XLA Modules:
  0.0 53.0 jit_solution(12347711464594993078)
XLA Ops:
  0.0 1.8 %shard_map.55 = (bf16[512,512]{1,0:T(8,128)(2,1)S(1)}, bf16[512,512]{1,0:T(8,128)(2,1)S(1)}, bf16[512,512]{1,0:T(8,128)(2,1)S(1)}, f32[784,128]{1,0:T(8,128)S(1)...) custom-call(bf16[512,512]{1,0:T(8,128)(2,1)} %q_hbm.1, ...), custom_call_target="tpu_custom_call" | custom-call | flops 134217728 | bytes 3670016 | tf_op jit(solution)/shard_map/pallas_call | solution.py:45
  1.8 3.0 %collective-permute-start.7 = (bf16[96,2048]{1,0:T(8,128)(2,1)S(1)}, bf16[96,2048]{1,0:T(8,128)(2,1)S(1)}, u32[]{:S(2)}, u32[]{:S(2)}) collective-permute-start(bf16[96,2048]{1,0:T(8,128)(2,1)S(1)} %get-tuple-element.59), channel_id=1, source_target_pairs={{0,2},{1,3},{2,0},{3,1},{4,6},{5,7},{6,4},{7,5},{8,10},{9,11},{10,... | collective-permute-start | bytes 1179656 | tf_op jit(solution)/shard_map/ppermute | solution.py:442
  4.9 2.0 %collective-permute-start = (bf16[784,128]{1,0:T(8,128)(2,1)S(1)}, bf16[784,128]{1,0:T(8,128)(2,1)S(1)}, u32[]{:S(2)}, u32[]{:S(2)}) collective-permute-start(bf16[784,128]{1,0:T(8,128)(2,1)S(1)} %get-tuple-element.37), channel_id=1, source_target_pairs={{0,4},{4,0},{8,12},{12,8},{16,20},{20,16},{24,28},{28,24},{1,5},{5... | collective-permute-start | bytes 602120 | tf_op jit(solution)/shard_map/ppermute | solution.py:442
  6.9 2.3 %shard_map.58 = (f32[4,128,128]{2,1,0:T(8,128)S(1)}, bf16[512,128]{1,0:T(8,128)(2,1)S(1)}, bf16[4,512,512]{2,1,0:T(8,128)(2,1)S(1)}, bf16[64,2048]{1,0:T(8,128)(2,1)S(1)}) custom-call(bf16[512,512]{1,0:T(8,128)(2,1)S(1)} %get-tuple-element.35.q_ref, bf16[512,512]{1,0:T(8,128)(2,1)S(1)} %get-tuple-element.44.k_ref, ...), custom_call_target="tpu_custom_call" | custom-call | flops 268435456 | bytes 3670016 | tf_op jit(solution)/shard_map/pallas_call | solution.py:45
  9.3 2.7 %collective-permute-done.got_ref.sums_got_ref = bf16[784,128]{1,0:T(8,128)(2,1)S(1)} collective-permute-done((bf16[784,128]{1,0:T(8,128)(2,1)S(1)}, bf16[784,128]{1,0:T(8,128)(2,1)S(1)}, u32[]{:S(2)}, u32[]{:S(2)}) %collective-permute-start) | collective-permute-done | bytes 200736 | tf_op jit(solution)/shard_map/ppermute | solution.py:442
  12.1 1.9 %collective-permute-start.1 = (bf16[784,128]{1,0:T(8,128)(2,1)S(1)}, bf16[784,128]{1,0:T(8,128)(2,1)S(1)}, u32[]{:S(2)}, u32[]{:S(2)}) collective-permute-start(bf16[784,128]{1,0:T(8,128)(2,1)S(1)} %get-tuple-element.39), channel_id=1, source_target_pairs={{0,8},{4,12},{8,0},{12,4},{16,24},{20,28},{24,16},{28,20},{1,9},{5... | collective-permute-start | bytes 602120 | tf_op jit(solution)/shard_map/ppermute | solution.py:442
  14.5 1.8 %collective-permute-start.4 = (bf16[512,128]{1,0:T(8,128)(2,1)S(1)}, bf16[512,128]{1,0:T(8,128)(2,1)S(1)}, u32[]{:S(2)}, u32[]{:S(2)}) collective-permute-start(bf16[512,128]{1,0:T(8,128)(2,1)S(1)} %get-tuple-element.47), channel_id=1, source_target_pairs={{0,8},{4,12},{8,0},{12,4},{16,24},{20,28},{24,16},{28,20},{1,9},{5... | collective-permute-start | bytes 393224 | tf_op jit(solution)/shard_map/ppermute | solution.py:442
  16.3 1.5 %collective-permute-start.10 = (bf16[96,2048]{1,0:T(8,128)(2,1)S(1)}, bf16[96,2048]{1,0:T(8,128)(2,1)S(1)}, u32[]{:S(2)}, u32[]{:S(2)}) collective-permute-start(bf16[96,2048]{1,0:T(8,128)(2,1)S(1)} %collective-permute-done.7.refs_0_), channel_id=1, source_target_pairs={{0,4},{4,0},{8,12},{12,8},{16,20},{20,16},{24,28},{28,24},{1,5},{5... | collective-permute-start | bytes 1179656 | tf_op jit(solution)/shard_map/ppermute | solution.py:442
  17.8 4.6 %collective-permute-done.8.refs_1_ = bf16[96,2048]{1,0:T(8,128)(2,1)S(1)} collective-permute-done((bf16[96,2048]{1,0:T(8,128)(2,1)S(1)}, bf16[96,2048]{1,0:T(8,128)(2,1)S(1)}, u32[]{:S(2)}, u32[]{:S(2)}) %collective-permute-start.8) | collective-permute-done | bytes 393248 | tf_op jit(solution)/shard_map/ppermute | solution.py:442
  22.4 1.8 %collective-permute-start.11 = (bf16[96,2048]{1,0:T(8,128)(2,1)S(1)}, bf16[96,2048]{1,0:T(8,128)(2,1)S(1)}, u32[]{:S(2)}, u32[]{:S(2)}) collective-permute-start(bf16[96,2048]{1,0:T(8,128)(2,1)S(1)} %collective-permute-done.8.refs_1_), channel_id=1, source_target_pairs={{0,4},{4,0},{8,12},{12,8},{16,20},{20,16},{24,28},{28,24},{1,5},{5... | collective-permute-start | bytes 1179656 | tf_op jit(solution)/shard_map/ppermute | solution.py:442
  24.2 1.5 %collective-permute-start.9 = (bf16[32,2048]{1,0:T(8,128)(2,1)S(1)}, bf16[32,2048]{1,0:T(8,128)(2,1)S(1)}, u32[]{:S(2)}, u32[]{:S(2)}) collective-permute-start(bf16[32,2048]{1,0:T(8,128)(2,1)S(1)} %get-tuple-element.61), channel_id=1, source_target_pairs={{0,2},{1,3},{2,0},{3,1},{4,6},{5,7},{6,4},{7,5},{8,10},{9,11},{10,... | collective-permute-start | bytes 393224 | tf_op jit(solution)/shard_map/ppermute | solution.py:442
  26.0 2.6 %collective-permute-start.5 = (bf16[512,128]{1,0:T(8,128)(2,1)S(1)}, bf16[512,128]{1,0:T(8,128)(2,1)S(1)}, u32[]{:S(2)}, u32[]{:S(2)}) collective-permute-start(bf16[512,128]{1,0:T(8,128)(2,1)S(1)} %get-tuple-element.54), channel_id=1, source_target_pairs={{0,16},{4,20},{8,24},{12,28},{16,0},{20,4},{24,8},{28,12},{1,17},{... | collective-permute-start | bytes 393224 | tf_op jit(solution)/shard_map/ppermute | solution.py:442
  28.6 0.5 %collective-permute-start.13 = (bf16[64,2048]{1,0:T(8,128)(2,1)S(1)}, bf16[64,2048]{1,0:T(8,128)(2,1)S(1)}, u32[]{:S(2)}, u32[]{:S(2)}) collective-permute-start(bf16[64,2048]{1,0:T(8,128)(2,1)S(1)} %get-tuple-element.62), channel_id=1, source_target_pairs={{0,2},{1,3},{2,0},{3,1},{4,6},{5,7},{6,4},{7,5},{8,10},{9,11},{10,... | collective-permute-start | bytes 786440 | tf_op jit(solution)/shard_map/ppermute | solution.py:442
  29.2 3.9 %collective-permute-start.2 = (bf16[272,128]{1,0:T(8,128)(2,1)S(1)}, bf16[272,128]{1,0:T(8,128)(2,1)S(1)}, u32[]{:S(2)}, u32[]{:S(2)}) collective-permute-start(bf16[272,128]{1,0:T(8,128)(2,1)S(1)} %get-tuple-element.42), channel_id=1, source_target_pairs={{0,16},{4,20},{8,24},{12,28},{16,0},{20,4},{24,8},{28,12},{1,17},{... | collective-permute-start | bytes 208904 | tf_op jit(solution)/shard_map/ppermute | solution.py:442
  33.1 1.4 %shard_map.63.refs_1_ = f32[512,256]{1,0:T(8,128)S(1)} custom-call(bf16[512,512]{1,0:T(8,128)(2,1)S(1)} %get-tuple-element.35.q_ref, bf16[512,512]{1,0:T(8,128)(2,1)S(1)} %get-tuple-element.44.k_ref, bf16[512,512]{1,0:T(8,128)(2,1)S(1)} %get-tuple-element.36.v_ref, bf16[4,512,512]{2,1,0:T(8,128)(2,1)S(1)} %get-tuple-element.52.paired_ref), custom_call_target="tpu_custom_call" | custom-call | flops 268435456 | bytes 3670016 | tf_op jit(solution)/shard_map/pallas_call | solution.py:45
  34.6 1.4 %shard_map.62.refs_0_ = f32[512,256]{1,0:T(8,128)S(1)} custom-call(bf16[512,512]{1,0:T(8,128)(2,1)S(1)} %get-tuple-element.35.q_ref, bf16[512,512]{1,0:T(8,128)(2,1)S(1)} %get-tuple-element.44.k_ref, bf16[512,512]{1,0:T(8,128)(2,1)S(1)} %get-tuple-element.36.v_ref, bf16[4,512,512]{2,1,0:T(8,128)(2,1)S(1)} %get-tuple-element.52.paired_ref), custom_call_target="tpu_custom_call" | custom-call | flops 268435456 | bytes 3670016 | tf_op jit(solution)/shard_map/pallas_call | solution.py:45
  36.6 1.1 %collective-permute-start.12 = (bf16[32,2048]{1,0:T(8,128)(2,1)S(1)}, bf16[32,2048]{1,0:T(8,128)(2,1)S(1)}, u32[]{:S(2)}, u32[]{:S(2)}) collective-permute-start(bf16[32,2048]{1,0:T(8,128)(2,1)S(1)} %collective-permute-done.9.refs_2_), channel_id=1, source_target_pairs={{0,8},{4,12},{8,0},{12,4},{16,24},{20,28},{24,16},{28,20},{1,9},{5... | collective-permute-start | bytes 393224 | tf_op jit(solution)/shard_map/ppermute | solution.py:442
  37.9 1.8 %shard_map.64.part_ref = f32[512,512]{1,0:T(8,128)S(1)} custom-call(bf16[512,512]{1,0:T(8,128)(2,1)S(1)} %get-tuple-element.35.q_ref, bf16[512,512]{1,0:T(8,128)(2,1)S(1)} %get-tuple-element.36.v_ref, bf16[4,128,128]{2,1,0:T(8,128)(2,1)S(1)} %get-tuple-element.51.gram_ref, f32[512,256]{1,0:T(8,128)S(1)} %shard_map.62.refs_0_, f32[512,256]{1,0:T(8,128)S(1)} %shard_map.63.refs_1_), custom_call_target="tpu_custom_call" | custom-call | flops 402653184 | bytes 2228224 | tf_op jit(solution)/shard_map/pallas_call | solution.py:45
  40.1 1.6 %collective-permute-start.14 = (bf16[128,512]{1,0:T(8,128)(2,1)S(1)}, bf16[128,512]{1,0:T(8,128)(2,1)S(1)}, u32[]{:S(2)}, u32[]{:S(2)}) collective-permute-start(bf16[128,512]{1,0:T(8,128)(2,1)S(1)} %get-tuple-element.64), channel_id=1, source_target_pairs={{0,2},{1,3},{2,0},{3,1},{4,6},{5,7},{6,4},{7,5},{8,10},{9,11},{10,... | collective-permute-start | bytes 393224 | tf_op jit(solution)/shard_map/ppermute | solution.py:442
  42.1 0.7 %shard_map.66 = (f32[128,2048]{1,0:T(8,128)S(1)}, f32[128,2048]{1,0:T(8,128)S(1)}) custom-call(bf16[512,2048]{1,0:T(8,128)(2,1)S(1)} %copy-done, bf16[128,512]{1,0:T(8,128)(2,1)S(1)} %get-tuple-element.55.refs_0_, bf16[128,512]{1,0:T(8,128)(2,1)S(1)} %get-tuple-element.56.refs_1_), custom_call_target="tpu_custom_call" | custom-call | flops 536870912 | bytes 2359296 | tf_op jit(solution)/shard_map/pallas_call | solution.py:45
  43.0 2.1 %collective-permute-done.14.came_ref = bf16[128,512]{1,0:T(8,128)(2,1)S(1)} collective-permute-done((bf16[128,512]{1,0:T(8,128)(2,1)S(1)}, bf16[128,512]{1,0:T(8,128)(2,1)S(1)}, u32[]{:S(2)}, u32[]{:S(2)}) %collective-permute-start.14) | collective-permute-done | bytes 131104 | tf_op jit(solution)/shard_map/ppermute | solution.py:442
  45.7 1.6 %collective-permute-start.6 = (bf16[128,512]{1,0:T(8,128)(2,1)S(1)}, bf16[128,512]{1,0:T(8,128)(2,1)S(1)}, u32[]{:S(2)}, u32[]{:S(2)}) collective-permute-start(bf16[128,512]{1,0:T(8,128)(2,1)S(1)} %get-tuple-element.58), channel_id=1, source_target_pairs={{0,2},{1,3},{2,0},{3,1},{4,6},{5,7},{6,4},{7,5},{8,10},{9,11},{10,... | collective-permute-start | bytes 393224 | tf_op jit(solution)/shard_map/ppermute | solution.py:442
  47.3 4.3 %collective-permute-done.6.came_ref = bf16[128,512]{1,0:T(8,128)(2,1)S(1)} collective-permute-done((bf16[128,512]{1,0:T(8,128)(2,1)S(1)}, bf16[128,512]{1,0:T(8,128)(2,1)S(1)}, u32[]{:S(2)}, u32[]{:S(2)}) %collective-permute-start.6) | collective-permute-done | bytes 131104 | tf_op jit(solution)/shard_map/ppermute | solution.py:442
  52.1 0.9 %add_convert_fusion = bf16[128,2048]{1,0:T(8,128)(2,1)} fusion(f32[128,2048]{1,0:T(8,128)S(1)} %shard_map.69, bf16[128,2048]{1,0:T(8,128)(2,1)S(1)} %collective-permute-done.15), kind=kLoop, calls=%fused_computation | loop fusion | flops 786432 | bytes 2097152 | tf_op jit(solution)/shard_map/convert_element_type | solution.py:506
  (29 shorter events, 3.9 us)
Async XLA Ops:
  1.8 14.4 %collective-permute-start.7 = (bf16[96,2048]{1,0:T(8,128)(2,1)S(1)}, bf16[96,2048]{1,0:T(8,128)(2,1)S(1)}, u32[]{:S(2)}, u32[]{:S(2)}) collective-permute-start(bf16[96,2048]{1,0:T(8,128)(2,1)S(1)} %get-tuple-element.59), channel_id=1, source_target_pairs={{0,2},{1,3},{2,0},{3,1},{4,6},{5,7},{6,4},{7,5},{8,10},{9,11},{10,... | collective-permute-start | bytes 1179656 | tf_op jit(solution)/shard_map/ppermute | solution.py:442
  4.8 17.5 %collective-permute-start.8 = (bf16[96,2048]{1,0:T(8,128)(2,1)S(1)}, bf16[96,2048]{1,0:T(8,128)(2,1)S(1)}, u32[]{:S(2)}, u32[]{:S(2)}) collective-permute-start(bf16[96,2048]{1,0:T(8,128)(2,1)S(1)} %get-tuple-element.60), channel_id=1, source_target_pairs={{0,2},{1,3},{2,0},{3,1},{4,6},{5,7},{6,4},{7,5},{8,10},{9,11},{10,... | collective-permute-start | bytes 1179656 | tf_op jit(solution)/shard_map/ppermute | solution.py:442
  4.9 7.1 %collective-permute-start = (bf16[784,128]{1,0:T(8,128)(2,1)S(1)}, bf16[784,128]{1,0:T(8,128)(2,1)S(1)}, u32[]{:S(2)}, u32[]{:S(2)}) collective-permute-start(bf16[784,128]{1,0:T(8,128)(2,1)S(1)} %get-tuple-element.37), channel_id=1, source_target_pairs={{0,4},{4,0},{8,12},{12,8},{16,20},{20,16},{24,28},{28,24},{1,5},{5... | collective-permute-start | bytes 602120 | tf_op jit(solution)/shard_map/ppermute | solution.py:442
  9.2 5.0 %collective-permute-start.3 = (bf16[512,128]{1,0:T(8,128)(2,1)S(1)}, bf16[512,128]{1,0:T(8,128)(2,1)S(1)}, u32[]{:S(2)}, u32[]{:S(2)}) collective-permute-start(bf16[512,128]{1,0:T(8,128)(2,1)S(1)} %get-tuple-element.45), channel_id=1, source_target_pairs={{0,4},{4,0},{8,12},{12,8},{16,20},{20,16},{24,28},{28,24},{1,5},{5... | collective-permute-start | bytes 393224 | tf_op jit(solution)/shard_map/ppermute | solution.py:442
  12.1 13.6 %collective-permute-start.1 = (bf16[784,128]{1,0:T(8,128)(2,1)S(1)}, bf16[784,128]{1,0:T(8,128)(2,1)S(1)}, u32[]{:S(2)}, u32[]{:S(2)}) collective-permute-start(bf16[784,128]{1,0:T(8,128)(2,1)S(1)} %get-tuple-element.39), channel_id=1, source_target_pairs={{0,8},{4,12},{8,0},{12,4},{16,24},{20,28},{24,16},{28,20},{1,9},{5... | collective-permute-start | bytes 602120 | tf_op jit(solution)/shard_map/ppermute | solution.py:442
  14.5 11.1 %collective-permute-start.4 = (bf16[512,128]{1,0:T(8,128)(2,1)S(1)}, bf16[512,128]{1,0:T(8,128)(2,1)S(1)}, u32[]{:S(2)}, u32[]{:S(2)}) collective-permute-start(bf16[512,128]{1,0:T(8,128)(2,1)S(1)} %get-tuple-element.47), channel_id=1, source_target_pairs={{0,8},{4,12},{8,0},{12,4},{16,24},{20,28},{24,16},{28,20},{1,9},{5... | collective-permute-start | bytes 393224 | tf_op jit(solution)/shard_map/ppermute | solution.py:442
  16.3 26.6 %collective-permute-start.10 = (bf16[96,2048]{1,0:T(8,128)(2,1)S(1)}, bf16[96,2048]{1,0:T(8,128)(2,1)S(1)}, u32[]{:S(2)}, u32[]{:S(2)}) collective-permute-start(bf16[96,2048]{1,0:T(8,128)(2,1)S(1)} %collective-permute-done.7.refs_0_), channel_id=1, source_target_pairs={{0,4},{4,0},{8,12},{12,8},{16,20},{20,16},{24,28},{28,24},{1,5},{5... | collective-permute-start | bytes 1179656 | tf_op jit(solution)/shard_map/ppermute | solution.py:442
  22.4 20.5 %collective-permute-start.11 = (bf16[96,2048]{1,0:T(8,128)(2,1)S(1)}, bf16[96,2048]{1,0:T(8,128)(2,1)S(1)}, u32[]{:S(2)}, u32[]{:S(2)}) collective-permute-start(bf16[96,2048]{1,0:T(8,128)(2,1)S(1)} %collective-permute-done.8.refs_1_), channel_id=1, source_target_pairs={{0,4},{4,0},{8,12},{12,8},{16,20},{20,16},{24,28},{28,24},{1,5},{5... | collective-permute-start | bytes 1179656 | tf_op jit(solution)/shard_map/ppermute | solution.py:442
  24.2 5.1 %collective-permute-start.9 = (bf16[32,2048]{1,0:T(8,128)(2,1)S(1)}, bf16[32,2048]{1,0:T(8,128)(2,1)S(1)}, u32[]{:S(2)}, u32[]{:S(2)}) collective-permute-start(bf16[32,2048]{1,0:T(8,128)(2,1)S(1)} %get-tuple-element.61), channel_id=1, source_target_pairs={{0,2},{1,3},{2,0},{3,1},{4,6},{5,7},{6,4},{7,5},{8,10},{9,11},{10,... | collective-permute-start | bytes 393224 | tf_op jit(solution)/shard_map/ppermute | solution.py:442
  26.0 13.7 %collective-permute-start.5 = (bf16[512,128]{1,0:T(8,128)(2,1)S(1)}, bf16[512,128]{1,0:T(8,128)(2,1)S(1)}, u32[]{:S(2)}, u32[]{:S(2)}) collective-permute-start(bf16[512,128]{1,0:T(8,128)(2,1)S(1)} %get-tuple-element.54), channel_id=1, source_target_pairs={{0,16},{4,20},{8,24},{12,28},{16,0},{20,4},{24,8},{28,12},{1,17},{... | collective-permute-start | bytes 393224 | tf_op jit(solution)/shard_map/ppermute | solution.py:442
  28.6 14.2 %collective-permute-start.13 = (bf16[64,2048]{1,0:T(8,128)(2,1)S(1)}, bf16[64,2048]{1,0:T(8,128)(2,1)S(1)}, u32[]{:S(2)}, u32[]{:S(2)}) collective-permute-start(bf16[64,2048]{1,0:T(8,128)(2,1)S(1)} %get-tuple-element.62), channel_id=1, source_target_pairs={{0,2},{1,3},{2,0},{3,1},{4,6},{5,7},{6,4},{7,5},{8,10},{9,11},{10,... | collective-permute-start | bytes 786440 | tf_op jit(solution)/shard_map/ppermute | solution.py:442
  29.2 7.3 %collective-permute-start.2 = (bf16[272,128]{1,0:T(8,128)(2,1)S(1)}, bf16[272,128]{1,0:T(8,128)(2,1)S(1)}, u32[]{:S(2)}, u32[]{:S(2)}) collective-permute-start(bf16[272,128]{1,0:T(8,128)(2,1)S(1)} %get-tuple-element.42), channel_id=1, source_target_pairs={{0,16},{4,20},{8,24},{12,28},{16,0},{20,4},{24,8},{28,12},{1,17},{... | collective-permute-start | bytes 208904 | tf_op jit(solution)/shard_map/ppermute | solution.py:442
  36.0 3.7 %copy-start.1 = (f32[512]{0:T(512)S(1)}, f32[512]{0:T(512)}, u32[]{:S(2)}) copy-start(f32[512]{0:T(512)} %param.8) | copy-start | bytes 6148
  36.6 6.3 %collective-permute-start.12 = (bf16[32,2048]{1,0:T(8,128)(2,1)S(1)}, bf16[32,2048]{1,0:T(8,128)(2,1)S(1)}, u32[]{:S(2)}, u32[]{:S(2)}) collective-permute-start(bf16[32,2048]{1,0:T(8,128)(2,1)S(1)} %collective-permute-done.9.refs_2_), channel_id=1, source_target_pairs={{0,8},{4,12},{8,0},{12,4},{16,24},{20,28},{24,16},{28,20},{1,9},{5... | collective-permute-start | bytes 393224 | tf_op jit(solution)/shard_map/ppermute | solution.py:442
  39.7 2.4 %copy-start = (bf16[512,2048]{1,0:T(8,128)(2,1)S(1)}, bf16[512,2048]{1,0:T(8,128)(2,1)}, u32[]{:S(2)}) copy-start(bf16[512,2048]{1,0:T(8,128)(2,1)} %w_ref.1) | copy-start | bytes 6291460
  40.1 5.0 %collective-permute-start.14 = (bf16[128,512]{1,0:T(8,128)(2,1)S(1)}, bf16[128,512]{1,0:T(8,128)(2,1)S(1)}, u32[]{:S(2)}, u32[]{:S(2)}) collective-permute-start(bf16[128,512]{1,0:T(8,128)(2,1)S(1)} %get-tuple-element.64), channel_id=1, source_target_pairs={{0,2},{1,3},{2,0},{3,1},{4,6},{5,7},{6,4},{7,5},{8,10},{9,11},{10,... | collective-permute-start | bytes 393224 | tf_op jit(solution)/shard_map/ppermute | solution.py:442
  45.6 6.4 %collective-permute-start.15 = (bf16[128,2048]{1,0:T(8,128)(2,1)S(1)}, bf16[128,2048]{1,0:T(8,128)(2,1)S(1)}, u32[]{:S(2)}, u32[]{:S(2)}) collective-permute-start(bf16[128,2048]{1,0:T(8,128)(2,1)S(1)} %shard_map.70), channel_id=1, source_target_pairs={{0,1},{1,0},{2,3},{3,2},{4,5},{5,4},{6,7},{7,6},{8,9},{9,8},{10,11... | collective-permute-start | bytes 1572872 | tf_op jit(solution)/shard_map/ppermute | solution.py:442
  45.7 5.9 %collective-permute-start.6 = (bf16[128,512]{1,0:T(8,128)(2,1)S(1)}, bf16[128,512]{1,0:T(8,128)(2,1)S(1)}, u32[]{:S(2)}, u32[]{:S(2)}) collective-permute-start(bf16[128,512]{1,0:T(8,128)(2,1)S(1)} %get-tuple-element.58), channel_id=1, source_target_pairs={{0,2},{1,3},{2,0},{3,1},{4,6},{5,7},{6,4},{7,5},{8,10},{9,11},{10,... | collective-permute-start | bytes 393224 | tf_op jit(solution)/shard_map/ppermute | solution.py:442
